TPU v7x, 128 devices: a whole 4x4x4 slice. The times are simulated.
128 devices in a mesh: ka: 64 (over y, z, x_lo, core), pa: 2 (over x_hi).
Axes of the slice: x: 4 (x_hi: 2, x_lo: 2; x = x_hi * 2 + x_lo), y: 4, z: 4, core: 2. Of those that a mesh axis runs over, the one named last changes fastest.
Arguments:
- conduction: bfloat16 [64, 48, 2048], P('ka'), may hold values from -6 to 6
- weighted: bfloat16 [64, 48, 2048], P('ka'), may hold values from -6 to 6
- valence: bfloat16 [64, 64, 2048], P('ka', None, 'pa'), may hold values from -0.015625 to 0.015625
- screening: bfloat16 [64, 2048, 2048], P('ka', None, 'pa'), may hold values from -0.125 to 0.125
- pair_transfer: int32 [64, 64], replicated, may hold values from 0 to 63, as said below
- owner_map: int32 [64], replicated, may hold values from 0 to 63, each once
Outputs:
- kernel_out: float32 [64, 48, 64], P('ka')
Inputs may be any that keep to these rules, and one draw needn't show every extreme that they name: pair_transfer[i, j] = (g_i - g_j) mod 64 for positions g of the k-points on a cyclic grid of 64 points (a permutation drawn from the seed), so each row and each column names every transfer once. `owner_map`: each transfer is held by exactly one slot.
All inputs are finite; a program needn't handle non-finite values.
Results may differ from a plain program's by a relative error of at most 0.0029.
Values may be sent and summed in bfloat16 or wider, within the bound.
No kernel may reach another device: no remote copies, remote signals or barrier semaphores. Data moves between devices by JAX's collectives and lax.ppermute only.
A program may use at most 128 MiB of HBM per device.

v0:
```python
import functools
import itertools

import jax
import jax.numpy as jnp
import numpy as np
from jax import lax
from jax.experimental import pallas as pl
from jax.experimental.pallas import tpu as pltpu
from jax.sharding import PartitionSpec as P


NY, NZ, NX = 4, 4, 4
CHIPS = 32
AXES = ("ka", "pa")
STEPS = {
    "y": ("y", 1, 3),
    "Y": ("y", 3, 1),
    "z": ("z", 1, 3),
    "Z": ("z", 3, 1),
    "x": ("x", 1, 3),
    "v": ("x", 1, 1),
}
SEQ = ("ZYzyx", "ZYyxz", "ZYxzy", "vZYzy")
HALF = CHIPS // 2


def device(y, z, x, core):
    return (((y * NZ + z) * 2 + x % 2) * 2 + core) * 2 + x // 2


def moved(masks):
    pairs = []
    for y, z, x, core in itertools.product(range(NY), range(NZ), range(NX), range(2)):
        my, mz, mx, mc = masks[core]
        pairs.append((device(y, z, x, core), device(y ^ my, z ^ mz, x ^ mx, core ^ mc)))
    return pairs


def send(value, masks):
    return lax.ppermute(value, AXES, moved(masks))


def step(value, letter):
    dim, *per_core = STEPS[letter]
    return send(value, [tuple(mask if dim == name else 0 for name in "yzx") + (0,) for mask in per_core])


def core_swap(value):
    return send(value, [(0, 0, 0, 1)] * 2)


def offsets(seq):
    table = np.zeros((2, CHIPS), np.int32)
    for core in range(2):
        for place in range(CHIPS):
            off = {"y": 0, "z": 0, "x": 0}
            for bit, letter in enumerate(seq):
                if place >> bit & 1:
                    off[STEPS[letter][0]] ^= STEPS[letter][1 + core]
            table[core, place] = off["y"] * 8 + off["z"] * 2 + (off["x"] & 1)
    return table


def screen_kernel(parts, rows, *refs):
    count = len(parts)
    given = [refs[11 * n : 11 * n + 11] for n in range(count)]
    screening = refs[11 * count : 11 * count + 2]
    out, mates, weights, dens, slots, msem, wsem, ssem = refs[11 * count + 2 :]
    column = pl.multiple_of(rows[192], 128)

    def load_slot(slot, cut):
        source = screening[slot].at[:, pl.ds(pl.multiple_of(cut * 256, 256), 256)]
        return pltpu.make_async_copy(source, slots.at[slot, cut], ssem.at[slot, cut])

    def load(n):
        for source, first, size in zip(given[n], (0, 8, 16, 24, 32, 48, 56), (8, 8, 8, 8, 16, 8, 8)):
            pltpu.make_async_copy(source, mates.at[n % 2, pl.ds(first, size)], msem.at[n % 2]).start()
        for k in range(4):
            pltpu.make_async_copy(given[n][7 + k], weights.at[n % 2, pl.ds(8 * k, 8)], wsem.at[n % 2]).start()

    def loaded(n):
        pltpu.make_async_copy(mates.at[n % 2], mates.at[n % 2], msem.at[n % 2]).wait()
        pltpu.make_async_copy(weights.at[n % 2], weights.at[n % 2], wsem.at[n % 2]).wait()

    load(0)
    for cut in range(4):
        for slot in range(2):
            load_slot(slot, cut).start()
    if count > 1:
        load(1)

    def pick(turn, slot, unit, cols):
        n = turn // 2
        where = rows[slot * 96 + parts[n] * 32 + (turn % 2) * HALF + unit]
        return mates[n % 2, where, :, cols]

    def build(turn, unit):
        weight = weights[(turn // 2) % 2, (turn % 2) * HALF + unit]
        for slot in range(2):
            here = pl.ds(pl.multiple_of(unit * 16, 16), 16)
            dens[turn % 2, slot, here, :] = pick(turn, slot, unit, slice(None)) * weight

    loaded(0)

    @pl.loop(0, HALF)
    def _(unit):
        build(0, unit)

    for turn in range(2 * count):
        if turn % 2 and turn + 1 < 2 * count:
            loaded((turn + 1) // 2)

        @pl.loop(0, 4)
        def _(cut):
            if turn == 0:
                for slot in range(2):
                    load_slot(slot, cut).wait()
            if turn + 1 < 2 * count:
                for unit in range(4):
                    build(turn + 1, cut * 4 + unit)
            cols = pl.ds(pl.multiple_of(cut * 256, 256), 256)
            here = pl.ds(pl.multiple_of(column + cut * 256, 128), 256)
            screened = [
                jnp.dot(dens[turn % 2, slot], slots[slot, cut], preferred_element_type=jnp.float32)
                for slot in range(2)
            ]
            for unit in range(HALF):
                block = slice(unit * 16, unit * 16 + 16)
                acc = None
                for slot in range(2):
                    term = pick(turn, slot, unit, here).astype(jnp.float32) * screened[slot][block]
                    acc = term if acc is None else acc + term
                out[turn // 2, (turn % 2) * HALF + unit, :, cols] = acc

        if turn % 2 and turn // 2 + 2 < count:
            load(turn // 2 + 2)


def screen(parts, rows, sources, wa, wb):
    vmem = pl.BlockSpec(memory_space=pltpu.VMEM)
    anywhere = pl.BlockSpec(memory_space=pl.ANY)
    count = len(parts)
    return pl.pallas_call(
        functools.partial(screen_kernel, parts),
        grid_spec=pltpu.PrefetchScalarGridSpec(
            num_scalar_prefetch=1,
            grid=(),
            in_specs=[anywhere] * (11 * count + 2),
            out_specs=vmem,
            scratch_shapes=[
                pltpu.VMEM((2, 2 * CHIPS, 16, 2048), jnp.bfloat16),
                pltpu.VMEM((2, CHIPS, 16, 2048), jnp.bfloat16),
                pltpu.VMEM((2, 2, HALF * 16, 2048), jnp.bfloat16),
                pltpu.VMEM((2, 4, 2048, 256), jnp.bfloat16),
                pltpu.SemaphoreType.DMA((2,)),
                pltpu.SemaphoreType.DMA((2,)),
                pltpu.SemaphoreType.DMA((2, 4)),
            ],
        ),
        out_shape=jax.ShapeDtypeStruct((count, CHIPS, 16, 1024), jnp.float32),
        compiler_params=pltpu.CompilerParams(vmem_limit_bytes=50 << 20),
        cost_estimate=pl.CostEstimate(flops=4_300_000_000 * count, bytes_accessed=8 << 20, transcendentals=0),
    )(rows, *sources, wa, wb)


def project_kernel(place, f0, f12, v0, v1, v2, v3, *outs):
    folded = (f0.at[0], f12.at[0], f12.at[1])

    def pick(where):
        slot, kind = lax.bitwise_and(where, 7), where // 8
        odd = lax.bitwise_and(kind, 1) == 1
        return jnp.where(kind < 2, jnp.where(odd, v1[slot], v0[slot]), jnp.where(odd, v3[slot], v2[slot]))

    for group in (1, 3, 2, 0):

        @pl.loop(0, 8, unroll=4)
        def _(unit):
            off = group * 8 + unit
            wide = jnp.concatenate([folded[part][place[part * 32 + off]] for part in range(3)], axis=0)
            high = wide.astype(jnp.bfloat16)
            low = (wide - high.astype(jnp.float32)).astype(jnp.bfloat16)
            left = jnp.concatenate([high, low], axis=0)
            bands = pick(place[96 + off])
            both = lax.dot_general(left, bands, (((1,), (1,)), ((), ())), preferred_element_type=jnp.float32)
            terms = both[:48] + both[48:]
            outs[group][unit] = jnp.concatenate([terms[:24], terms[24:]], axis=1)


def project(place, folded, val):
    vmem = pl.BlockSpec(memory_space=pltpu.VMEM)
    return pl.pallas_call(
        project_kernel,
        grid_spec=pltpu.PrefetchScalarGridSpec(
            num_scalar_prefetch=1, grid=(), in_specs=[vmem] * 6, out_specs=[vmem] * 4
        ),
        out_shape=[jax.ShapeDtypeStruct((8, 24, 128), jnp.float32)] * 4,
        compiler_params=pltpu.CompilerParams(vmem_limit_bytes=14 << 20),
        cost_estimate=pl.CostEstimate(flops=800_000_000, bytes_accessed=10 << 20, transcendentals=0),
    )(place, *folded, *val)


def spread(parts, dim, masks):
    moves = []
    for mask in masks:
        one = tuple(mask if dim == name else 0 for name in "yzx") + (0,)
        moves.append(send(parts[mask], [one] * 2))
    return (parts[0] + moves[0]) + (moves[1] + moves[2])


def lookup(keys, table):
    spots = jnp.arange(table.shape[-1], dtype=jnp.int32)
    return jnp.sum(jnp.where(keys[..., None] == spots, table[..., None, :], 0), axis=-1)


def tables(chip, core, pa, pair_transfer, owner_map):
    owned = lax.dynamic_slice_in_dim(owner_map, chip * 2, 2)
    owned = jnp.where(core == 0, owned, owned[::-1])
    columns = jnp.arange(pair_transfer.shape[1], dtype=jnp.int32)
    partner = jnp.sum(jnp.where(pair_transfer[None] == owned[:, None, None], columns, 0), axis=2)
    offs = np.stack([offsets(seq) for seq in SEQ])
    place = np.argsort(offs, axis=-1).astype(np.int32)
    mine = lambda table: jnp.where(core == 0, table[:, 0], table[:, 1])
    home = lax.bitwise_xor(mine(offs[:3]), chip) * 2 + core
    mates = lookup(jnp.broadcast_to(home, (2, 3, CHIPS)), partner[:, None, :])
    key = lax.bitwise_xor(mates & 1, core) * CHIPS + lax.bitwise_xor(mates >> 1, chip)
    both = np.stack([np.concatenate([place[:3, c], CHIPS + place[:3, 1 - c]], -1) for c in (0, 1)], 1)
    rows = lookup(key, mine(both)[None])
    rows = jnp.concatenate([rows.reshape(-1), (pa * 1024).astype(jnp.int32)[None]])
    return rows, mine(place).reshape(-1)


def shards(conduction, weighted, valence, screening, pair_transfer, owner_map):
    ka, pa = lax.axis_index("ka"), lax.axis_index("pa")
    chip, core = ka // 2, ka % 2
    rows, place = tables(chip, core, pa, pair_transfer, owner_map)
    mine = screening[0]

    stream = jnp.concatenate([conduction, weighted], axis=1)
    val = [valence]
    for turn in range(2):
        moves = [step(stream, SEQ[0][turn]), step(val[0], SEQ[3][turn])]
        stream, val, moves = lax.optimization_barrier((stream, val, moves))
        stream = jnp.concatenate([stream, moves[0]], axis=0)
        val = [jnp.concatenate([val[0], moves[1]], axis=0)]
    parts = [slice(16 * part, 16 * part + 16) for part in range(3)]
    streams = [jnp.concatenate([stream[:, :48][:, cut], stream[:, 48:][:, cut]], axis=1) for cut in parts]
    moves = [step(block, SEQ[k][2]) for k, block in enumerate(streams)]
    val_move = step(val[0], SEQ[3][2])
    streams, moves = lax.optimization_barrier((streams, moves))
    cond = [[jnp.concatenate([one[:, :16], two[:, :16]], axis=0)] for one, two in zip(streams, moves)]
    weights = [[jnp.concatenate([one[:, 16:], two[:, 16:]], axis=0)] for one, two in zip(streams, moves)]

    def onward(pieces, source, turn):
        for k, held in enumerate(pieces):
            held.append(step(held[source], SEQ[k][turn]))

    onward(cond, 0, 3)
    onward(cond, 0, 4)
    onward(cond, 1, 4)
    onward(weights, 0, 3)
    onward(weights, 0, 4)
    onward(weights, 1, 4)
    val = jnp.concatenate([val[0], val_move], axis=0)
    swapped = core_swap(mine)
    val_next, val_far = step(val, SEQ[3][3]), step(val, SEQ[3][4])
    others = []
    for held in cond:
        both = [jnp.concatenate(held[:2], axis=0), held[2], held[3]]
        others.append([core_swap(block) for block in both])
    inputs = [held + other + weight for held, other, weight in zip(cond, others, weights)]
    first = screen((0,), rows, inputs[0], mine, swapped)
    first, val_next = lax.optimization_barrier((first, val_next))
    val_last = step(val_next, SEQ[3][4])
    folded = [first, screen((1, 2), rows, inputs[1] + inputs[2], mine, swapped)]
    folded, val_last = lax.optimization_barrier((folded, val_last))
    terms = project(place, folded, (val, val_next, val_far, val_last))
    terms = spread(terms, "y", (1, 3, 2))
    terms = terms.reshape(4, 2, 24, 128)
    terms = spread([terms[k] for k in range(4)], "z", (1, 3, 2))
    near = send(terms[1], [(0, 0, 1, 0)] * 2)
    wrap = send(terms[1], [(0, 0, 3, 0)] * 2)
    across = send(terms[0], [(0, 0, 2, 0)] * 2)
    total = (terms[0] + across) + (near + wrap)
    return jnp.concatenate([total[:, :64], total[:, 64:]], axis=0)[None]


def solution(mesh):
    in_specs = (
        P("ka", None, None),
        P("ka", None, None),
        P("ka", None, "pa"),
        P("ka", None, "pa"),
        P(),
        P(),
    )
    out_specs = P("ka", None, None)
    return jax.shard_map(shards, mesh=mesh, in_specs=in_specs, out_specs=out_specs, check_vma=False)
```

profile of v0, /device:TPU:0, one launch (start us, length us, event | category | flops | bytes accessed | tf_op | source)
XLA Modules:
  0.0 185.2 jit_solution(10121225718055261299)
XLA Ops:
  0.0 1.0 constant_dynamic-update-slice_fusion.1
  1.0 0.9 constant_dynamic-update-slice_fusion
  1.9 4.2 %collective-permute-start = (bf16[1,96,2048]{2,1,0:T(8,128)(2,1)S(1)}, bf16[1,96,2048]{2,1,0:T(8,128)(2,1)S(1)}, u32[]{:S(2)}, u32[]{:S(2)}) collective-permute-start(bf16[1,96,2048]{2,1,0:T(8,128)(2,1)S(1)} %constant_dynamic-update-slice_fusion), channel_id=1, source_target_pairs={{0,24},{2,10},{4,28},{6,14},{1,25},{3,11},{5,29},{7,15},{8,16},{10... | collective-permute-start | bytes 1179656 | tf_op jit(solution)/shard_map/ppermute | solution.py:41
  6.2 1.5 collective-permute-start.1
  7.6 3.7 %collective-permute-done.1 = bf16[1,64,1024]{2,1,0:T(8,128)(2,1)S(1)} collective-permute-done((bf16[1,64,1024]{2,1,0:T(8,128)(2,1)}, bf16[1,64,1024]{2,1,0:T(8,128)(2,1)S(1)}, u32[]{:S(2)}, u32[]{:S(2)}) %collective-permute-start.1) | collective-permute-done | bytes 131104 | tf_op jit(solution)/shard_map/ppermute | solution.py:41
  12.0 3.1 %collective-permute-start.2 = (bf16[2,96,2048]{2,1,0:T(8,128)(2,1)S(1)}, bf16[2,96,2048]{2,1,0:T(8,128)(2,1)S(1)}, u32[]{:S(2)}, u32[]{:S(2)}) collective-permute-start(bf16[2,96,2048]{2,1,0:T(8,128)(2,1)S(1)} %constant_dynamic-update-slice_fusion.2), channel_id=1, source_target_pairs={{0,96},{2,34},{4,100},{6,38},{1,97},{3,35},{5,101},{7,39},{8,104},... | collective-permute-start | bytes 2359304 | tf_op jit(solution)/shard_map/ppermute | solution.py:41
  15.1 3.3 %collective-permute-start.3 = (bf16[2,64,1024]{2,1,0:T(8,128)(2,1)S(1)}, bf16[2,64,1024]{2,1,0:T(8,128)(2,1)S(1)}, u32[]{:S(2)}, u32[]{:S(2)}) collective-permute-start(bf16[2,64,1024]{2,1,0:T(8,128)(2,1)S(1)} %constant_dynamic-update-slice_fusion.4), channel_id=1, source_target_pairs={{0,24},{2,10},{4,28},{6,14},{1,25},{3,11},{5,29},{7,15},{8,16},{10... | collective-permute-start | bytes 786440 | tf_op jit(solution)/shard_map/ppermute | solution.py:41
  18.4 4.4 %collective-permute-done.3 = bf16[2,64,1024]{2,1,0:T(8,128)(2,1)S(1)} collective-permute-done((bf16[2,64,1024]{2,1,0:T(8,128)(2,1)S(1)}, bf16[2,64,1024]{2,1,0:T(8,128)(2,1)S(1)}, u32[]{:S(2)}, u32[]{:S(2)}) %collective-permute-start.3) | collective-permute-done | bytes 262176 | tf_op jit(solution)/shard_map/ppermute | solution.py:41
  22.8 2.5 %collective-permute-done.2 = bf16[2,96,2048]{2,1,0:T(8,128)(2,1)S(1)} collective-permute-done((bf16[2,96,2048]{2,1,0:T(8,128)(2,1)S(1)}, bf16[2,96,2048]{2,1,0:T(8,128)(2,1)S(1)}, u32[]{:S(2)}, u32[]{:S(2)}) %collective-permute-start.2) | collective-permute-done | bytes 786464 | tf_op jit(solution)/shard_map/ppermute | solution.py:41
  25.6 1.6 collective-permute-start.6
  27.8 2.0 %collective-permute-start.16 = (bf16[2048,1024]{1,0:T(8,128)(2,1)}, bf16[2048,1024]{1,0:T(8,128)(2,1)}, u32[]{:S(2)}, u32[]{:S(2)}) collective-permute-start(bf16[2048,1024]{1,0:T(8,128)(2,1)} %bitcast.1.refs_11_.refs_22_), channel_id=1, source_target_pairs={{0,2},{2,0},{4,6},{6,4},{1,3},{3,1},{5,7},{7,5},{8,10},{10,8},{12,... | collective-permute-start | bytes 12582920 | tf_op jit(solution)/shard_map/ppermute | solution.py:41
  29.9 0.9 collective-permute-start.17
  30.7 4.2 %collective-permute-done.6 = bf16[4,32,2048]{2,1,0:T(8,128)(2,1)S(1)} collective-permute-done((bf16[4,32,2048]{2,1,0:T(8,128)(2,1)S(1)}, bf16[4,32,2048]{2,1,0:T(8,128)(2,1)S(1)}, u32[]{:S(2)}, u32[]{:S(2)}) %collective-permute-start.6) | collective-permute-done | bytes 524320 | tf_op jit(solution)/shard_map/ppermute | solution.py:41
  34.9 5.6 %collective-permute-done.5 = bf16[4,32,2048]{2,1,0:T(8,128)(2,1)S(1)} collective-permute-done((bf16[4,32,2048]{2,1,0:T(8,128)(2,1)S(1)}, bf16[4,32,2048]{2,1,0:T(8,128)(2,1)S(1)}, u32[]{:S(2)}, u32[]{:S(2)}) %collective-permute-start.5) | collective-permute-done | bytes 524320 | tf_op jit(solution)/shard_map/ppermute | solution.py:41
  41.3 2.0 %collective-permute-start.28 = (bf16[8,16,2048]{2,1,0:T(8,128)(2,1)S(1)}, bf16[8,16,2048]{2,1,0:T(8,128)(2,1)S(1)}, u32[]{:S(2)}, u32[]{:S(2)}) collective-permute-start(bf16[8,16,2048]{2,1,0:T(8,128)(2,1)S(1)} %pad_maximum_fusion.11.refs_11_), channel_id=1, source_target_pairs={{0,8},{2,26},{4,12},{6,30},{1,9},{3,27},{5,13},{7,31},{8,0},{10,18... | collective-permute-start | bytes 1572872 | tf_op jit(solution)/shard_map/ppermute | solution.py:41
  43.6 1.7 collective-permute-start.29
  45.3 4.6 %collective-permute-done.34.refs_19_ = bf16[8,16,2048]{2,1,0:T(8,128)(2,1)S(1)} collective-permute-done((bf16[8,16,2048]{2,1,0:T(8,128)(2,1)S(1)}, bf16[8,16,2048]{2,1,0:T(8,128)(2,1)S(1)}, u32[]{:S(2)}, u32[]{:S(2)}) %collective-permute-start.34) | collective-permute-done | bytes 524320 | tf_op jit(solution)/shard_map/ppermute | solution.py:41
  49.9 0.8 collective-permute-start.25
  50.7 1.2 collective-permute-start.26
  51.9 3.6 %collective-permute-done.28.refs_12_ = bf16[8,16,2048]{2,1,0:T(8,128)(2,1)S(1)} collective-permute-done((bf16[8,16,2048]{2,1,0:T(8,128)(2,1)S(1)}, bf16[8,16,2048]{2,1,0:T(8,128)(2,1)S(1)}, u32[]{:S(2)}, u32[]{:S(2)}) %collective-permute-start.28) | collective-permute-done | bytes 524320 | tf_op jit(solution)/shard_map/ppermute | solution.py:41
  56.3 0.8 collective-permute-start.19
  57.5 1.5 collective-permute-done.25.refs_8_
  59.5 1.6 collective-permute-done.26.refs_9_
  61.1 0.8 collective-permute-start.14
  62.0 3.6 %collective-permute-done.19.refs_1_ = bf16[8,16,2048]{2,1,0:T(8,128)(2,1)} collective-permute-done((bf16[8,16,2048]{2,1,0:T(8,128)(2,1)S(1)}, bf16[8,16,2048]{2,1,0:T(8,128)(2,1)}, u32[]{:S(2)}, u32[]{:S(2)}) %collective-permute-start.19) | collective-permute-done | bytes 524320 | tf_op jit(solution)/shard_map/ppermute | solution.py:41
  66.8 1.1 collective-permute-start.8
  68.8 2.3 %collective-permute-done.14.refs_9_ = bf16[8,16,2048]{2,1,0:T(8,128)(2,1)S(1)} collective-permute-done((bf16[8,16,2048]{2,1,0:T(8,128)(2,1)S(1)}, bf16[8,16,2048]{2,1,0:T(8,128)(2,1)S(1)}, u32[]{:S(2)}, u32[]{:S(2)}) %collective-permute-start.14) | collective-permute-done | bytes 524320 | tf_op jit(solution)/shard_map/ppermute | solution.py:41
  71.6 3.2 %collective-permute-done.7.refs_1_ = bf16[8,16,2048]{2,1,0:T(8,128)(2,1)S(1)} collective-permute-done((bf16[8,16,2048]{2,1,0:T(8,128)(2,1)S(1)}, bf16[8,16,2048]{2,1,0:T(8,128)(2,1)S(1)}, u32[]{:S(2)}, u32[]{:S(2)}) %collective-permute-start.7) | collective-permute-done | bytes 524320 | tf_op jit(solution)/shard_map/ppermute | solution.py:41
  75.0 1.7 collective-permute-done.8.refs_2_
  76.7 3.7 %collective-permute-done.36.refs_21_ = bf16[8,16,2048]{2,1,0:T(8,128)(2,1)S(1)} collective-permute-done((bf16[8,16,2048]{2,1,0:T(8,128)(2,1)}, bf16[8,16,2048]{2,1,0:T(8,128)(2,1)S(1)}, u32[]{:S(2)}, u32[]{:S(2)}) %collective-permute-start.36) | collective-permute-done | bytes 524320 | tf_op jit(solution)/shard_map/ppermute | solution.py:41
  80.4 5.6 %collective-permute-done.30.refs_14_ = bf16[8,16,2048]{2,1,0:T(8,128)(2,1)S(1)} collective-permute-done((bf16[8,16,2048]{2,1,0:T(8,128)(2,1)}, bf16[8,16,2048]{2,1,0:T(8,128)(2,1)S(1)}, u32[]{:S(2)}, u32[]{:S(2)}) %collective-permute-start.30) | collective-permute-done | bytes 524320 | tf_op jit(solution)/shard_map/ppermute | solution.py:41
  86.0 0.8 copy-done.44
  86.8 0.8 collective-permute-start.15
  87.7 1.0 constant_dynamic-update-slice_fusion.10
  88.7 1.0 constant_dynamic-update-slice_fusion.9
  89.7 1.1 constant_dynamic-update-slice_fusion.8.v0
  92.0 1.3 collective-permute-start.9
  93.2 3.0 %collective-permute-done.15.refs_10_ = bf16[8,16,2048]{2,1,0:T(8,128)(2,1)S(1)} collective-permute-done((bf16[8,16,2048]{2,1,0:T(8,128)(2,1)}, bf16[8,16,2048]{2,1,0:T(8,128)(2,1)S(1)}, u32[]{:S(2)}, u32[]{:S(2)}) %collective-permute-start.15) | collective-permute-done | bytes 524320 | tf_op jit(solution)/shard_map/ppermute | solution.py:41
  96.6 1.1 pad_maximum_fusion.2
  97.7 4.3 %collective-permute-done.9.refs_3_ = bf16[8,16,2048]{2,1,0:T(8,128)(2,1)} collective-permute-done((bf16[8,16,2048]{2,1,0:T(8,128)(2,1)S(1)}, bf16[8,16,2048]{2,1,0:T(8,128)(2,1)}, u32[]{:S(2)}, u32[]{:S(2)}) %collective-permute-start.9) | collective-permute-done | bytes 524320 | tf_op jit(solution)/shard_map/ppermute | solution.py:41
  102.0 1.0 collective-permute-start.31
  103.0 2.3 %pad_maximum_fusion.1 = bf16[16,16,2048]{2,1,0:T(8,128)(2,1)} fusion(bf16[8,16,2048]{2,1,0:T(8,128)(2,1)} %collective-permute-done.19.refs_1_, bf16[4,16,2048]{2,1,0:T(8,128)(2,1)S(1)} %copy-done.15, bf16[4,16,2048]{2,1,0:T(8,128)(2,1)S(1)} %copy-done.13), kind=kLoop, calls=%fused_computation.1 | loop fusion | flops 1048576 | bytes 2097152 | tf_op jit(solution)/shard_map/concatenate | solution.py:269
  105.4 1.2 collective-permute-done.18.v1
  108.4 1.0 copy-done.3
  109.4 12.4 %shard_map.118.f0 = f32[1,32,16,1024]{3,2,1,0:T(8,128)} custom-call(s32[193]{0:T(256)S(1)} %pad_add_fusion.rows, bf16[8,16,2048]{2,1,0:T(8,128)(2,1)S(1)} %pad_maximum_fusion.6.refs_0_, bf16[8,16,2048]{2,1,0:T(8,128)(2,1)S(1)} %collective-permute-done.7.refs_1_, bf16[8,16,2048]{2,1,0:T(8,128)(2,1)S(1)} %collective-permute-done.8.refs_2_, ...), custom_call_target="tpu_custom_call" | custom-call | flops 4300000256 | bytes 8388608 | tf_op jit(solution)/shard_map/pallas_call | solution.py:144
  122.1 1.8 collective-permute-start.38
  124.1 1.2 copy-done.5
  125.2 1.0 copy-done.7
  126.3 1.0 copy-done.9
  127.3 18.6 %shard_map.119.f12 = f32[2,32,16,1024]{3,2,1,0:T(8,128)} custom-call(s32[193]{0:T(256)S(1)} %pad_add_fusion.rows, bf16[8,16,2048]{2,1,0:T(8,128)(2,1)S(1)} %copy-done.7, bf16[8,16,2048]{2,1,0:T(8,128)(2,1)} %collective-permute-done.19.refs_1_, bf16[8,16,2048]{2,1,0:T(8,128)(2,1)} %collective-permute-done.20.refs_2_, bf16[8,16,2048]{2,1,0:T(8,128)(2,1)S(1)} %copy-done.9, ...), custom_call_target="tpu_custom_call" | custom-call | flops 8600000512 | bytes 8388608 | tf_op jit(solution)/shard_map/pallas_call | solution.py:144
  146.0 2.3 %collective-permute-done.38.v2 = bf16[8,64,1024]{2,1,0:T(8,128)(2,1)} collective-permute-done((bf16[8,64,1024]{2,1,0:T(8,128)(2,1)S(1)}, bf16[8,64,1024]{2,1,0:T(8,128)(2,1)}, u32[]{:S(2)}, u32[]{:S(2)}) %collective-permute-start.38) | collective-permute-done | bytes 1048608 | tf_op jit(solution)/shard_map/ppermute | solution.py:41
  148.3 2.2 %copy-done.1 = f32[2,32,16,1024]{3,2,1,0:T(8,128)S(1)} copy-done((f32[2,32,16,1024]{3,2,1,0:T(8,128)S(1)}, f32[2,32,16,1024]{3,2,1,0:T(8,128)}, u32[]{:S(2)}) %copy-start.1) | copy-done | bytes 4194328
  150.5 5.9 %shard_map.120 = (f32[8,24,128]{2,1,0:T(8,128)S(1)}, f32[8,24,128]{2,1,0:T(8,128)S(1)}, f32[8,24,128]{2,1,0:T(8,128)S(1)}, f32[8,24,128]{2,1,0:T(8,128)S(1)}) custom-call(s32[128]{0:T(128)S(1)} %reshape.27.place, f32[1,32,16,1024]{3,2,1,0:T(8,128)S(1)} %copy-done, f32[2,32,16,1024]{3,2,1,0:T(8,128)S(1)} %copy-done.1, ...), custom_call_target="tpu_custom_call" | custom-call | flops 800000000 | bytes 10485760 | tf_op jit(solution)/shard_map/pallas_call | solution.py:192
  156.7 4.1 %collective-permute-start.40 = (f32[8,24,128]{2,1,0:T(8,128)S(1)}, f32[8,24,128]{2,1,0:T(8,128)S(1)}, u32[]{:S(2)}, u32[]{:S(2)}) collective-permute-start(f32[8,24,128]{2,1,0:T(8,128)S(1)} %get-tuple-element.49), channel_id=1, source_target_pairs={{0,96},{2,98},{4,100},{6,102},{1,97},{3,99},{5,101},{7,103},{8,104... | collective-permute-start | bytes 294920 | tf_op jit(solution)/shard_map/ppermute | solution.py:41
  160.8 1.4 collective-permute-start.41
  162.1 3.1 %collective-permute-done.40 = f32[8,24,128]{2,1,0:T(8,128)S(1)} collective-permute-done((f32[8,24,128]{2,1,0:T(8,128)S(1)}, f32[8,24,128]{2,1,0:T(8,128)S(1)}, u32[]{:S(2)}, u32[]{:S(2)}) %collective-permute-start.40) | collective-permute-done | bytes 98336 | tf_op jit(solution)/shard_map/ppermute | solution.py:41
  165.2 1.8 collective-permute-done.41
  167.4 3.2 %collective-permute-start.43 = (f32[2,24,128]{2,1,0:T(8,128)S(1)}, f32[2,24,128]{2,1,0:T(8,128)S(1)}, u32[]{:S(2)}, u32[]{:S(2)}) collective-permute-start(f32[2,24,128]{2,1,0:T(8,128)S(1)} %get-tuple-element.70), channel_id=1, source_target_pairs={{0,24},{2,26},{4,28},{6,30},{1,25},{3,27},{5,29},{7,31},{8,16},{10... | collective-permute-start | bytes 73736 | tf_op jit(solution)/shard_map/ppermute | solution.py:41
  170.6 1.3 collective-permute-start.44
  172.4 3.5 %collective-permute-done.44 = f32[2,24,128]{2,1,0:T(8,128)S(1)} collective-permute-done((f32[2,24,128]{2,1,0:T(8,128)S(1)}, f32[2,24,128]{2,1,0:T(8,128)S(1)}, u32[]{:S(2)}, u32[]{:S(2)}) %collective-permute-start.44) | collective-permute-done | bytes 24608 | tf_op jit(solution)/shard_map/ppermute | solution.py:41
  176.0 3.0 %collective-permute-start.45 = (f32[24,128]{1,0:T(8,128)S(1)}, f32[24,128]{1,0:T(8,128)S(1)}, u32[]{:S(2)}, u32[]{:S(2)}) collective-permute-start(f32[24,128]{1,0:T(8,128)S(1)} %get-tuple-element.72), channel_id=1, source_target_pairs={{0,1},{2,3},{4,5},{6,7},{1,0},{3,2},{5,4},{7,6},{8,9},{10,11},{12,... | collective-permute-start | bytes 36872 | tf_op jit(solution)/shard_map/ppermute | solution.py:41
  180.1 1.1 collective-permute-done.45
  181.2 1.4 collective-permute-done.46
  182.7 1.8 collective-permute-done.47
  (177 shorter events, 13.6 us)
Async XLA Ops:
  0.0 15.1 %copy-start.29 = (bf16[1,64,1024]{2,1,0:T(8,128)(2,1)S(1)}, bf16[1,64,1024]{2,1,0:T(8,128)(2,1)}, u32[]{:S(2)}) copy-start(bf16[1,64,1024]{2,1,0:T(8,128)(2,1)} %param.14) | copy-start | bytes 393220
  1.9 10.0 %collective-permute-start = (bf16[1,96,2048]{2,1,0:T(8,128)(2,1)S(1)}, bf16[1,96,2048]{2,1,0:T(8,128)(2,1)S(1)}, u32[]{:S(2)}, u32[]{:S(2)}) collective-permute-start(bf16[1,96,2048]{2,1,0:T(8,128)(2,1)S(1)} %constant_dynamic-update-slice_fusion), channel_id=1, source_target_pairs={{0,24},{2,10},{4,28},{6,14},{1,25},{3,11},{5,29},{7,15},{8,16},{10... | collective-permute-start | bytes 1179656 | tf_op jit(solution)/shard_map/ppermute | solution.py:41
  6.2 5.2 %collective-permute-start.1 = (bf16[1,64,1024]{2,1,0:T(8,128)(2,1)}, bf16[1,64,1024]{2,1,0:T(8,128)(2,1)S(1)}, u32[]{:S(2)}, u32[]{:S(2)}) collective-permute-start(bf16[1,64,1024]{2,1,0:T(8,128)(2,1)} %param.14), channel_id=1, source_target_pairs={{0,4},{2,6},{4,0},{6,2},{1,5},{3,7},{5,1},{7,3},{8,12},{10,14},{12... | collective-permute-start | bytes 393224 | tf_op jit(solution)/shard_map/ppermute | solution.py:41
  12.0 13.3 %collective-permute-start.2 = (bf16[2,96,2048]{2,1,0:T(8,128)(2,1)S(1)}, bf16[2,96,2048]{2,1,0:T(8,128)(2,1)S(1)}, u32[]{:S(2)}, u32[]{:S(2)}) collective-permute-start(bf16[2,96,2048]{2,1,0:T(8,128)(2,1)S(1)} %constant_dynamic-update-slice_fusion.2), channel_id=1, source_target_pairs={{0,96},{2,34},{4,100},{6,38},{1,97},{3,35},{5,101},{7,39},{8,104},... | collective-permute-start | bytes 2359304 | tf_op jit(solution)/shard_map/ppermute | solution.py:41
  15.1 14.7 %copy-start.20 = (bf16[2,64,1024]{2,1,0:T(8,128)(2,1)}, bf16[2,64,1024]{2,1,0:T(8,128)(2,1)S(1)}, u32[]{:S(2)}) copy-start(bf16[2,64,1024]{2,1,0:T(8,128)(2,1)S(1)} %constant_dynamic-update-slice_fusion.4) | copy-start | bytes 786436
  15.1 7.7 %collective-permute-start.3 = (bf16[2,64,1024]{2,1,0:T(8,128)(2,1)S(1)}, bf16[2,64,1024]{2,1,0:T(8,128)(2,1)S(1)}, u32[]{:S(2)}, u32[]{:S(2)}) collective-permute-start(bf16[2,64,1024]{2,1,0:T(8,128)(2,1)S(1)} %constant_dynamic-update-slice_fusion.4), channel_id=1, source_target_pairs={{0,24},{2,10},{4,28},{6,14},{1,25},{3,11},{5,29},{7,15},{8,16},{10... | collective-permute-start | bytes 786440 | tf_op jit(solution)/shard_map/ppermute | solution.py:41
  25.6 9.3 %collective-permute-start.6 = (bf16[4,32,2048]{2,1,0:T(8,128)(2,1)S(1)}, bf16[4,32,2048]{2,1,0:T(8,128)(2,1)S(1)}, u32[]{:S(2)}, u32[]{:S(2)}) collective-permute-start(bf16[4,32,2048]{2,1,0:T(8,128)(2,1)S(1)} %pad_maximum_fusion.5), channel_id=1, source_target_pairs={{0,4},{2,7},{4,0},{6,3},{1,5},{3,6},{5,1},{7,2},{8,12},{10,15},{12... | collective-permute-start | bytes 1572872 | tf_op jit(solution)/shard_map/ppermute | solution.py:41
  27.2 13.2 %collective-permute-start.5 = (bf16[4,32,2048]{2,1,0:T(8,128)(2,1)S(1)}, bf16[4,32,2048]{2,1,0:T(8,128)(2,1)S(1)}, u32[]{:S(2)}, u32[]{:S(2)}) collective-permute-start(bf16[4,32,2048]{2,1,0:T(8,128)(2,1)S(1)} %pad_maximum_fusion.4), channel_id=1, source_target_pairs={{0,32},{2,98},{4,36},{6,102},{1,33},{3,99},{5,37},{7,103},{8,40},{... | collective-permute-start | bytes 1572872 | tf_op jit(solution)/shard_map/ppermute | solution.py:41
  27.7 12.7 %collective-permute-start.4 = (bf16[4,32,2048]{2,1,0:T(8,128)(2,1)S(1)}, bf16[4,32,2048]{2,1,0:T(8,128)(2,1)S(1)}, u32[]{:S(2)}, u32[]{:S(2)}) collective-permute-start(bf16[4,32,2048]{2,1,0:T(8,128)(2,1)S(1)} %pad_maximum_fusion.3), channel_id=1, source_target_pairs={{0,8},{2,26},{4,12},{6,30},{1,9},{3,27},{5,13},{7,31},{8,0},{10,18... | collective-permute-start | bytes 1572872 | tf_op jit(solution)/shard_map/ppermute | solution.py:41
  27.8 80.1 %collective-permute-start.16 = (bf16[2048,1024]{1,0:T(8,128)(2,1)}, bf16[2048,1024]{1,0:T(8,128)(2,1)}, u32[]{:S(2)}, u32[]{:S(2)}) collective-permute-start(bf16[2048,1024]{1,0:T(8,128)(2,1)} %bitcast.1.refs_11_.refs_22_), channel_id=1, source_target_pairs={{0,2},{2,0},{4,6},{6,4},{1,3},{3,1},{5,7},{7,5},{8,10},{10,8},{12,... | collective-permute-start | bytes 12582920 | tf_op jit(solution)/shard_map/ppermute | solution.py:41
  29.9 13.7 %collective-permute-start.17 = (bf16[4,64,1024]{2,1,0:T(8,128)(2,1)S(1)}, bf16[4,64,1024]{2,1,0:T(8,128)(2,1)S(1)}, u32[]{:S(2)}, u32[]{:S(2)}) collective-permute-start(bf16[4,64,1024]{2,1,0:T(8,128)(2,1)S(1)} %pad_maximum_fusion.8), channel_id=1, source_target_pairs={{0,96},{2,34},{4,100},{6,38},{1,97},{3,35},{5,101},{7,39},{8,104},... | collective-permute-start | bytes 1572872 | tf_op jit(solution)/shard_map/ppermute | solution.py:41
  40.6 9.3 %collective-permute-start.34 = (bf16[8,16,2048]{2,1,0:T(8,128)(2,1)S(1)}, bf16[8,16,2048]{2,1,0:T(8,128)(2,1)S(1)}, u32[]{:S(2)}, u32[]{:S(2)}) collective-permute-start(bf16[8,16,2048]{2,1,0:T(8,128)(2,1)S(1)} %pad_maximum_fusion.12.refs_18_), channel_id=1, source_target_pairs={{0,8},{2,26},{4,12},{6,30},{1,9},{3,27},{5,13},{7,31},{8,0},{10,18... | collective-permute-start | bytes 1572872 | tf_op jit(solution)/shard_map/ppermute | solution.py:41
  40.7 10.0 %collective-permute-start.35 = (bf16[8,16,2048]{2,1,0:T(8,128)(2,1)S(1)}, bf16[8,16,2048]{2,1,0:T(8,128)(2,1)S(1)}, u32[]{:S(2)}, u32[]{:S(2)}) collective-permute-start(bf16[8,16,2048]{2,1,0:T(8,128)(2,1)S(1)} %pad_maximum_fusion.12.refs_18_), channel_id=1, source_target_pairs={{0,32},{2,98},{4,36},{6,102},{1,33},{3,99},{5,37},{7,103},{8,40},{... | collective-permute-start | bytes 1572872 | tf_op jit(solution)/shard_map/ppermute | solution.py:41
  41.3 14.2 %collective-permute-start.28 = (bf16[8,16,2048]{2,1,0:T(8,128)(2,1)S(1)}, bf16[8,16,2048]{2,1,0:T(8,128)(2,1)S(1)}, u32[]{:S(2)}, u32[]{:S(2)}) collective-permute-start(bf16[8,16,2048]{2,1,0:T(8,128)(2,1)S(1)} %pad_maximum_fusion.11.refs_11_), channel_id=1, source_target_pairs={{0,8},{2,26},{4,12},{6,30},{1,9},{3,27},{5,13},{7,31},{8,0},{10,18... | collective-permute-start | bytes 1572872 | tf_op jit(solution)/shard_map/ppermute | solution.py:41
  43.6 13.8 %copy-start.6 = (bf16[8,16,2048]{2,1,0:T(8,128)(2,1)}, bf16[8,16,2048]{2,1,0:T(8,128)(2,1)S(1)}, u32[]{:S(2)}) copy-start(bf16[8,16,2048]{2,1,0:T(8,128)(2,1)S(1)} %pad_maximum_fusion.9.refs_0_) | copy-start | bytes 1572868
  43.6 22.0 %copy-start.26 = (bf16[4,64,1024]{2,1,0:T(8,128)(2,1)}, bf16[4,64,1024]{2,1,0:T(8,128)(2,1)S(1)}, u32[]{:S(2)}) copy-start(bf16[4,64,1024]{2,1,0:T(8,128)(2,1)S(1)} %collective-permute-done.17) | copy-start | bytes 1572868
  43.6 13.8 %collective-permute-start.29 = (bf16[8,16,2048]{2,1,0:T(8,128)(2,1)S(1)}, bf16[8,16,2048]{2,1,0:T(8,128)(2,1)S(1)}, u32[]{:S(2)}, u32[]{:S(2)}) collective-permute-start(bf16[8,16,2048]{2,1,0:T(8,128)(2,1)S(1)} %pad_maximum_fusion.11.refs_11_), channel_id=1, source_target_pairs={{0,32},{2,98},{4,36},{6,102},{1,33},{3,99},{5,37},{7,103},{8,40},{... | collective-permute-start | bytes 1572872 | tf_op jit(solution)/shard_map/ppermute | solution.py:41
  49.9 16.2 %copy-start.38 = (bf16[8,16,2048]{2,1,0:T(8,128)(2,1)}, bf16[8,16,2048]{2,1,0:T(8,128)(2,1)S(1)}, u32[]{:S(2)}) copy-start(bf16[8,16,2048]{2,1,0:T(8,128)(2,1)S(1)} %collective-permute-done.34.refs_19_) | copy-start | bytes 1572868
  49.9 9.2 %collective-permute-start.25 = (bf16[8,16,2048]{2,1,0:T(8,128)(2,1)S(1)}, bf16[8,16,2048]{2,1,0:T(8,128)(2,1)S(1)}, u32[]{:S(2)}, u32[]{:S(2)}) collective-permute-start(bf16[8,16,2048]{2,1,0:T(8,128)(2,1)S(1)} %pad_maximum_fusion.10.refs_7_), channel_id=1, source_target_pairs={{0,4},{2,7},{4,0},{6,3},{1,5},{3,6},{5,1},{7,2},{8,12},{10,15},{12... | collective-permute-start | bytes 1572872 | tf_op jit(solution)/shard_map/ppermute | solution.py:41
  50.7 15.3 %copy-start.39 = (bf16[8,16,2048]{2,1,0:T(8,128)(2,1)}, bf16[8,16,2048]{2,1,0:T(8,128)(2,1)S(1)}, u32[]{:S(2)}) copy-start(bf16[8,16,2048]{2,1,0:T(8,128)(2,1)S(1)} %collective-permute-done.35.refs_20_) | copy-start | bytes 1572868
  50.7 10.4 %collective-permute-start.26 = (bf16[8,16,2048]{2,1,0:T(8,128)(2,1)S(1)}, bf16[8,16,2048]{2,1,0:T(8,128)(2,1)S(1)}, u32[]{:S(2)}, u32[]{:S(2)}) collective-permute-start(bf16[8,16,2048]{2,1,0:T(8,128)(2,1)S(1)} %pad_maximum_fusion.10.refs_7_), channel_id=1, source_target_pairs={{0,8},{2,26},{4,12},{6,30},{1,9},{3,27},{5,13},{7,31},{8,0},{10,18... | collective-permute-start | bytes 1572872 | tf_op jit(solution)/shard_map/ppermute | solution.py:41
  56.3 9.3 %collective-permute-start.19 = (bf16[8,16,2048]{2,1,0:T(8,128)(2,1)S(1)}, bf16[8,16,2048]{2,1,0:T(8,128)(2,1)}, u32[]{:S(2)}, u32[]{:S(2)}) collective-permute-start(bf16[8,16,2048]{2,1,0:T(8,128)(2,1)S(1)} %pad_maximum_fusion.9.refs_0_), channel_id=1, source_target_pairs={{0,4},{2,7},{4,0},{6,3},{1,5},{3,6},{5,1},{7,2},{8,12},{10,15},{12... | collective-permute-start | bytes 1572872 | tf_op jit(solution)/shard_map/ppermute | solution.py:41
  57.2 28.8 %copy-start.16 = (bf16[4,16,2048]{2,1,0:T(8,128)(2,1)}, bf16[4,16,2048]{2,1,0:T(8,128)(2,1)S(1)}, u32[]{:S(2)}) copy-start(bf16[4,16,2048]{2,1,0:T(8,128)(2,1)S(1)} %get-tuple-element.66) | copy-start | bytes 786436
  57.3 28.8 %copy-start.18 = (bf16[4,16,2048]{2,1,0:T(8,128)(2,1)}, bf16[4,16,2048]{2,1,0:T(8,128)(2,1)S(1)}, u32[]{:S(2)}) copy-start(bf16[4,16,2048]{2,1,0:T(8,128)(2,1)S(1)} %get-tuple-element.80) | copy-start | bytes 786436
  57.3 14.3 %copy-start.35 = (s32[3,32]{1,0:T(4,128)S(1)}, s32[3,32]{1,0:T(4,128)}, u32[]{:S(2)}) copy-start(s32[3,32]{1,0:T(4,128)} %constant.53.clone) | copy-start | bytes 1156
  57.3 14.3 %copy-start.36 = (s32[3,32]{1,0:T(4,128)S(1)}, s32[3,32]{1,0:T(4,128)}, u32[]{:S(2)}) copy-start(s32[3,32]{1,0:T(4,128)} %constant.54.clone) | copy-start | bytes 1156
  57.3 17.6 %copy-start.30 = (s32[64,64]{1,0:T(8,128)S(1)}, s32[64,64]{1,0:T(8,128)}, u32[]{:S(2)}) copy-start(s32[64,64]{1,0:T(8,128)} %param.16) | copy-start | bytes 49156
  57.4 9.4 %collective-permute-start.20 = (bf16[8,16,2048]{2,1,0:T(8,128)(2,1)S(1)}, bf16[8,16,2048]{2,1,0:T(8,128)(2,1)}, u32[]{:S(2)}, u32[]{:S(2)}) collective-permute-start(bf16[8,16,2048]{2,1,0:T(8,128)(2,1)S(1)} %pad_maximum_fusion.9.refs_0_), channel_id=1, source_target_pairs={{0,8},{2,26},{4,12},{6,30},{1,9},{3,27},{5,13},{7,31},{8,0},{10,18... | collective-permute-start | bytes 1572872 | tf_op jit(solution)/shard_map/ppermute | solution.py:41
  59.1 9.3 %collective-permute-start.13 = (bf16[8,16,2048]{2,1,0:T(8,128)(2,1)S(1)}, bf16[8,16,2048]{2,1,0:T(8,128)(2,1)}, u32[]{:S(2)}, u32[]{:S(2)}) collective-permute-start(bf16[8,16,2048]{2,1,0:T(8,128)(2,1)S(1)} %pad_maximum_fusion.7.refs_7_), channel_id=1, source_target_pairs={{0,32},{2,98},{4,36},{6,102},{1,33},{3,99},{5,37},{7,103},{8,40},{... | collective-permute-start | bytes 1572872 | tf_op jit(solution)/shard_map/ppermute | solution.py:41
  61.1 10.0 %collective-permute-start.14 = (bf16[8,16,2048]{2,1,0:T(8,128)(2,1)S(1)}, bf16[8,16,2048]{2,1,0:T(8,128)(2,1)S(1)}, u32[]{:S(2)}, u32[]{:S(2)}) collective-permute-start(bf16[8,16,2048]{2,1,0:T(8,128)(2,1)S(1)} %pad_maximum_fusion.7.refs_7_), channel_id=1, source_target_pairs={{0,4},{2,7},{4,0},{6,3},{1,5},{3,6},{5,1},{7,2},{8,12},{10,15},{12... | collective-permute-start | bytes 1572872 | tf_op jit(solution)/shard_map/ppermute | solution.py:41
  65.6 9.2 %collective-permute-start.7 = (bf16[8,16,2048]{2,1,0:T(8,128)(2,1)S(1)}, bf16[8,16,2048]{2,1,0:T(8,128)(2,1)S(1)}, u32[]{:S(2)}, u32[]{:S(2)}) collective-permute-start(bf16[8,16,2048]{2,1,0:T(8,128)(2,1)S(1)} %pad_maximum_fusion.6.refs_0_), channel_id=1, source_target_pairs={{0,32},{2,98},{4,36},{6,102},{1,33},{3,99},{5,37},{7,103},{8,40},{... | collective-permute-start | bytes 1572872 | tf_op jit(solution)/shard_map/ppermute | solution.py:41
  66.8 9.9 %collective-permute-start.8 = (bf16[8,16,2048]{2,1,0:T(8,128)(2,1)S(1)}, bf16[8,16,2048]{2,1,0:T(8,128)(2,1)S(1)}, u32[]{:S(2)}, u32[]{:S(2)}) collective-permute-start(bf16[8,16,2048]{2,1,0:T(8,128)(2,1)S(1)} %pad_maximum_fusion.6.refs_0_), channel_id=1, source_target_pairs={{0,4},{2,7},{4,0},{6,3},{1,5},{3,6},{5,1},{7,2},{8,12},{10,15},{12... | collective-permute-start | bytes 1572872 | tf_op jit(solution)/shard_map/ppermute | solution.py:41
  68.3 12.0 %collective-permute-start.36 = (bf16[8,16,2048]{2,1,0:T(8,128)(2,1)}, bf16[8,16,2048]{2,1,0:T(8,128)(2,1)S(1)}, u32[]{:S(2)}, u32[]{:S(2)}) collective-permute-start(bf16[8,16,2048]{2,1,0:T(8,128)(2,1)} %copy-done.38), channel_id=1, source_target_pairs={{0,32},{2,98},{4,36},{6,102},{1,33},{3,99},{5,37},{7,103},{8,40},{... | collective-permute-start | bytes 1572872 | tf_op jit(solution)/shard_map/ppermute | solution.py:41
  71.1 14.9 %copy-start.22 = (bf16[8,16,2048]{2,1,0:T(8,128)(2,1)}, bf16[8,16,2048]{2,1,0:T(8,128)(2,1)S(1)}, u32[]{:S(2)}) copy-start(bf16[8,16,2048]{2,1,0:T(8,128)(2,1)S(1)} %collective-permute-done.14.refs_9_) | copy-start | bytes 1572868
  71.1 14.9 %collective-permute-start.30 = (bf16[8,16,2048]{2,1,0:T(8,128)(2,1)}, bf16[8,16,2048]{2,1,0:T(8,128)(2,1)S(1)}, u32[]{:S(2)}, u32[]{:S(2)}) collective-permute-start(bf16[8,16,2048]{2,1,0:T(8,128)(2,1)} %copy-done.27), channel_id=1, source_target_pairs={{0,32},{2,98},{4,36},{6,102},{1,33},{3,99},{5,37},{7,103},{8,40},{... | collective-permute-start | bytes 1572872 | tf_op jit(solution)/shard_map/ppermute | solution.py:41
  74.8 16.1 %collective-permute-start.32 = (bf16[8,16,2048]{2,1,0:T(8,128)(2,1)}, bf16[8,16,2048]{2,1,0:T(8,128)(2,1)S(1)}, u32[]{:S(2)}, u32[]{:S(2)}) collective-permute-start(bf16[8,16,2048]{2,1,0:T(8,128)(2,1)} %copy-done.40), channel_id=1, source_target_pairs={{0,2},{2,0},{4,6},{6,4},{1,3},{3,1},{5,7},{7,5},{8,10},{10,8},{12,... | collective-permute-start | bytes 1572872 | tf_op jit(solution)/shard_map/ppermute | solution.py:41
  76.7 15.1 %collective-permute-start.27 = (bf16[8,16,2048]{2,1,0:T(8,128)(2,1)}, bf16[8,16,2048]{2,1,0:T(8,128)(2,1)S(1)}, u32[]{:S(2)}, u32[]{:S(2)}) collective-permute-start(bf16[8,16,2048]{2,1,0:T(8,128)(2,1)} %copy-done.41), channel_id=1, source_target_pairs={{0,8},{2,26},{4,12},{6,30},{1,9},{3,27},{5,13},{7,31},{8,0},{10,18... | collective-permute-start | bytes 1572872 | tf_op jit(solution)/shard_map/ppermute | solution.py:41
  80.4 11.6 %collective-permute-start.21 = (bf16[8,16,2048]{2,1,0:T(8,128)(2,1)}, bf16[8,16,2048]{2,1,0:T(8,128)(2,1)S(1)}, u32[]{:S(2)}, u32[]{:S(2)}) collective-permute-start(bf16[8,16,2048]{2,1,0:T(8,128)(2,1)} %collective-permute-done.19.refs_1_), channel_id=1, source_target_pairs={{0,8},{2,26},{4,12},{6,30},{1,9},{3,27},{5,13},{7,31},{8,0},{10,18... | collective-permute-start | bytes 1572872 | tf_op jit(solution)/shard_map/ppermute | solution.py:41
  86.8 9.4 %collective-permute-start.15 = (bf16[8,16,2048]{2,1,0:T(8,128)(2,1)}, bf16[8,16,2048]{2,1,0:T(8,128)(2,1)S(1)}, u32[]{:S(2)}, u32[]{:S(2)}) collective-permute-start(bf16[8,16,2048]{2,1,0:T(8,128)(2,1)} %collective-permute-done.13.refs_8_), channel_id=1, source_target_pairs={{0,4},{2,7},{4,0},{6,3},{1,5},{3,6},{5,1},{7,2},{8,12},{10,15},{12... | collective-permute-start | bytes 1572872 | tf_op jit(solution)/shard_map/ppermute | solution.py:41
  91.7 14.9 %collective-permute-start.18 = (bf16[8,64,1024]{2,1,0:T(8,128)(2,1)S(1)}, bf16[8,64,1024]{2,1,0:T(8,128)(2,1)}, u32[]{:S(2)}, u32[]{:S(2)}) collective-permute-start(bf16[8,64,1024]{2,1,0:T(8,128)(2,1)S(1)} %constant_dynamic-update-slice_fusion.8.v0), channel_id=1, source_target_pairs={{0,8},{2,26},{4,12},{6,30},{1,9},{3,27},{5,13},{7,31},{8,0},{10,18... | collective-permute-start | bytes 3145736 | tf_op jit(solution)/shard_map/ppermute | solution.py:41
  91.8 14.8 %copy-start.46 = (bf16[8,16,2048]{2,1,0:T(8,128)(2,1)}, bf16[8,16,2048]{2,1,0:T(8,128)(2,1)S(1)}, u32[]{:S(2)}) copy-start(bf16[8,16,2048]{2,1,0:T(8,128)(2,1)S(1)} %collective-permute-done.27.refs_10_) | copy-start | bytes 1572868
  91.9 14.8 %collective-permute-start.10 = (bf16[16,16,2048]{2,1,0:T(8,128)(2,1)S(1)}, bf16[16,16,2048]{2,1,0:T(8,128)(2,1)}, u32[]{:S(2)}, u32[]{:S(2)}) collective-permute-start(bf16[16,16,2048]{2,1,0:T(8,128)(2,1)S(1)} %pad_maximum_fusion), channel_id=1, source_target_pairs={{0,2},{2,0},{4,6},{6,4},{1,3},{3,1},{5,7},{7,5},{8,10},{10,8},{12,... | collective-permute-start | bytes 3145736 | tf_op jit(solution)/shard_map/ppermute | solution.py:41
  92.0 10.0 %collective-permute-start.9 = (bf16[8,16,2048]{2,1,0:T(8,128)(2,1)S(1)}, bf16[8,16,2048]{2,1,0:T(8,128)(2,1)}, u32[]{:S(2)}, u32[]{:S(2)}) collective-permute-start(bf16[8,16,2048]{2,1,0:T(8,128)(2,1)S(1)} %collective-permute-done.7.refs_1_), channel_id=1, source_target_pairs={{0,4},{2,7},{4,0},{6,3},{1,5},{3,6},{5,1},{7,2},{8,12},{10,15},{12... | collective-permute-start | bytes 1572872 | tf_op jit(solution)/shard_map/ppermute | solution.py:41
  96.2 6.7 %collective-permute-start.11 = (bf16[8,16,2048]{2,1,0:T(8,128)(2,1)S(1)}, bf16[8,16,2048]{2,1,0:T(8,128)(2,1)S(1)}, u32[]{:S(2)}, u32[]{:S(2)}) collective-permute-start(bf16[8,16,2048]{2,1,0:T(8,128)(2,1)S(1)} %collective-permute-done.8.refs_2_), channel_id=1, source_target_pairs={{0,2},{2,0},{4,6},{6,4},{1,3},{3,1},{5,7},{7,5},{8,10},{10,8},{12,... | collective-permute-start | bytes 1572872 | tf_op jit(solution)/shard_map/ppermute | solution.py:41
  102.0 20.1 %collective-permute-start.31 = (bf16[16,16,2048]{2,1,0:T(8,128)(2,1)}, bf16[16,16,2048]{2,1,0:T(8,128)(2,1)}, u32[]{:S(2)}, u32[]{:S(2)}) collective-permute-start(bf16[16,16,2048]{2,1,0:T(8,128)(2,1)} %pad_maximum_fusion.2), channel_id=1, source_target_pairs={{0,2},{2,0},{4,6},{6,4},{1,3},{3,1},{5,7},{7,5},{8,10},{10,8},{12,... | collective-permute-start | bytes 3145736 | tf_op jit(solution)/shard_map/ppermute | solution.py:41
  102.9 4.9 %collective-permute-start.12 = (bf16[8,16,2048]{2,1,0:T(8,128)(2,1)}, bf16[8,16,2048]{2,1,0:T(8,128)(2,1)}, u32[]{:S(2)}, u32[]{:S(2)}) collective-permute-start(bf16[8,16,2048]{2,1,0:T(8,128)(2,1)} %collective-permute-done.9.refs_3_), channel_id=1, source_target_pairs={{0,2},{2,0},{4,6},{6,4},{1,3},{3,1},{5,7},{7,5},{8,10},{10,8},{12,... | collective-permute-start | bytes 1572872 | tf_op jit(solution)/shard_map/ppermute | solution.py:41
  106.6 17.5 %collective-permute-start.22 = (bf16[16,16,2048]{2,1,0:T(8,128)(2,1)}, bf16[16,16,2048]{2,1,0:T(8,128)(2,1)}, u32[]{:S(2)}, u32[]{:S(2)}) collective-permute-start(bf16[16,16,2048]{2,1,0:T(8,128)(2,1)} %pad_maximum_fusion.1), channel_id=1, source_target_pairs={{0,2},{2,0},{4,6},{6,4},{1,3},{3,1},{5,7},{7,5},{8,10},{10,8},{12,... | collective-permute-start | bytes 3145736 | tf_op jit(solution)/shard_map/ppermute | solution.py:41
  106.6 15.2 %collective-permute-start.23 = (bf16[8,16,2048]{2,1,0:T(8,128)(2,1)}, bf16[8,16,2048]{2,1,0:T(8,128)(2,1)}, u32[]{:S(2)}, u32[]{:S(2)}) collective-permute-start(bf16[8,16,2048]{2,1,0:T(8,128)(2,1)} %collective-permute-done.20.refs_2_), channel_id=1, source_target_pairs={{0,2},{2,0},{4,6},{6,4},{1,3},{3,1},{5,7},{7,5},{8,10},{10,8},{12,... | collective-permute-start | bytes 1572872 | tf_op jit(solution)/shard_map/ppermute | solution.py:41
  107.7 16.2 %copy-start.32 = (s32[4,32]{1,0:T(4,128)S(1)}, s32[4,32]{1,0:T(4,128)}, u32[]{:S(2)}) copy-start(s32[4,32]{1,0:T(4,128)} %constant.58.clone) | copy-start | bytes 1540
  107.7 16.2 %copy-start.31 = (s32[4,32]{1,0:T(4,128)S(1)}, s32[4,32]{1,0:T(4,128)}, u32[]{:S(2)}) copy-start(s32[4,32]{1,0:T(4,128)} %constant.57.clone) | copy-start | bytes 1540
  107.8 16.2 %collective-permute-start.33 = (bf16[8,16,2048]{2,1,0:T(8,128)(2,1)}, bf16[8,16,2048]{2,1,0:T(8,128)(2,1)}, u32[]{:S(2)}, u32[]{:S(2)}) collective-permute-start(bf16[8,16,2048]{2,1,0:T(8,128)(2,1)} %copy-done.44), channel_id=1, source_target_pairs={{0,2},{2,0},{4,6},{6,4},{1,3},{3,1},{5,7},{7,5},{8,10},{10,8},{12,... | collective-permute-start | bytes 1572872 | tf_op jit(solution)/shard_map/ppermute | solution.py:41
  107.9 16.2 %collective-permute-start.24 = (bf16[8,16,2048]{2,1,0:T(8,128)(2,1)}, bf16[8,16,2048]{2,1,0:T(8,128)(2,1)}, u32[]{:S(2)}, u32[]{:S(2)}) collective-permute-start(bf16[8,16,2048]{2,1,0:T(8,128)(2,1)} %copy-done.8), channel_id=1, source_target_pairs={{0,2},{2,0},{4,6},{6,4},{1,3},{3,1},{5,7},{7,5},{8,10},{10,8},{12,... | collective-permute-start | bytes 1572872 | tf_op jit(solution)/shard_map/ppermute | solution.py:41
  121.8 24.1 %collective-permute-start.37 = (bf16[8,64,1024]{2,1,0:T(8,128)(2,1)}, bf16[8,64,1024]{2,1,0:T(8,128)(2,1)S(1)}, u32[]{:S(2)}, u32[]{:S(2)}) collective-permute-start(bf16[8,64,1024]{2,1,0:T(8,128)(2,1)} %collective-permute-done.18.v1), channel_id=1, source_target_pairs={{0,32},{2,98},{4,36},{6,102},{1,33},{3,99},{5,37},{7,103},{8,40},{... | collective-permute-start | bytes 3145736 | tf_op jit(solution)/shard_map/ppermute | solution.py:41
  122.1 26.2 %collective-permute-start.38 = (bf16[8,64,1024]{2,1,0:T(8,128)(2,1)S(1)}, bf16[8,64,1024]{2,1,0:T(8,128)(2,1)}, u32[]{:S(2)}, u32[]{:S(2)}) collective-permute-start(bf16[8,64,1024]{2,1,0:T(8,128)(2,1)S(1)} %constant_dynamic-update-slice_fusion.8.v0), channel_id=1, source_target_pairs={{0,32},{2,98},{4,36},{6,102},{1,33},{3,99},{5,37},{7,103},{8,40},{... | collective-permute-start | bytes 3145736 | tf_op jit(solution)/shard_map/ppermute | solution.py:41
  124.0 24.2 %copy-start = (f32[1,32,16,1024]{3,2,1,0:T(8,128)S(1)}, f32[1,32,16,1024]{3,2,1,0:T(8,128)}, u32[]{:S(2)}) copy-start(f32[1,32,16,1024]{3,2,1,0:T(8,128)} %shard_map.118.f0) | copy-start | bytes 6291460
  156.4 5.8 %collective-permute-start.39 = (f32[8,24,128]{2,1,0:T(8,128)S(1)}, f32[8,24,128]{2,1,0:T(8,128)S(1)}, u32[]{:S(2)}, u32[]{:S(2)}) collective-permute-start(f32[8,24,128]{2,1,0:T(8,128)S(1)} %get-tuple-element.48), channel_id=1, source_target_pairs={{0,32},{2,34},{4,36},{6,38},{1,33},{3,35},{5,37},{7,39},{8,40},{10... | collective-permute-start | bytes 294920 | tf_op jit(solution)/shard_map/ppermute | solution.py:41
  156.7 8.6 %collective-permute-start.40 = (f32[8,24,128]{2,1,0:T(8,128)S(1)}, f32[8,24,128]{2,1,0:T(8,128)S(1)}, u32[]{:S(2)}, u32[]{:S(2)}) collective-permute-start(f32[8,24,128]{2,1,0:T(8,128)S(1)} %get-tuple-element.49), channel_id=1, source_target_pairs={{0,96},{2,98},{4,100},{6,102},{1,97},{3,99},{5,101},{7,103},{8,104... | collective-permute-start | bytes 294920 | tf_op jit(solution)/shard_map/ppermute | solution.py:41
  160.8 6.3 %collective-permute-start.41 = (f32[8,24,128]{2,1,0:T(8,128)S(1)}, f32[8,24,128]{2,1,0:T(8,128)S(1)}, u32[]{:S(2)}, u32[]{:S(2)}) collective-permute-start(f32[8,24,128]{2,1,0:T(8,128)S(1)} %get-tuple-element.50), channel_id=1, source_target_pairs={{0,64},{2,66},{4,68},{6,70},{1,65},{3,67},{5,69},{7,71},{8,72},{10... | collective-permute-start | bytes 294920 | tf_op jit(solution)/shard_map/ppermute | solution.py:41
  167.1 4.8 %collective-permute-start.42 = (f32[2,24,128]{2,1,0:T(8,128)S(1)}, f32[2,24,128]{2,1,0:T(8,128)S(1)}, u32[]{:S(2)}, u32[]{:S(2)}) collective-permute-start(f32[2,24,128]{2,1,0:T(8,128)S(1)} %get-tuple-element.71), channel_id=1, source_target_pairs={{0,8},{2,10},{4,12},{6,14},{1,9},{3,11},{5,13},{7,15},{8,0},{10,2}... | collective-permute-start | bytes 73736 | tf_op jit(solution)/shard_map/ppermute | solution.py:41
  167.4 5.0 %collective-permute-start.43 = (f32[2,24,128]{2,1,0:T(8,128)S(1)}, f32[2,24,128]{2,1,0:T(8,128)S(1)}, u32[]{:S(2)}, u32[]{:S(2)}) collective-permute-start(f32[2,24,128]{2,1,0:T(8,128)S(1)} %get-tuple-element.70), channel_id=1, source_target_pairs={{0,24},{2,26},{4,28},{6,30},{1,25},{3,27},{5,29},{7,31},{8,16},{10... | collective-permute-start | bytes 73736 | tf_op jit(solution)/shard_map/ppermute | solution.py:41
  170.6 5.3 %collective-permute-start.44 = (f32[2,24,128]{2,1,0:T(8,128)S(1)}, f32[2,24,128]{2,1,0:T(8,128)S(1)}, u32[]{:S(2)}, u32[]{:S(2)}) collective-permute-start(f32[2,24,128]{2,1,0:T(8,128)S(1)} %get-tuple-element.69), channel_id=1, source_target_pairs={{0,16},{2,18},{4,20},{6,22},{1,17},{3,19},{5,21},{7,23},{8,24},{10... | collective-permute-start | bytes 73736 | tf_op jit(solution)/shard_map/ppermute | solution.py:41
  176.0 5.3 %collective-permute-start.45 = (f32[24,128]{1,0:T(8,128)S(1)}, f32[24,128]{1,0:T(8,128)S(1)}, u32[]{:S(2)}, u32[]{:S(2)}) collective-permute-start(f32[24,128]{1,0:T(8,128)S(1)} %get-tuple-element.72), channel_id=1, source_target_pairs={{0,1},{2,3},{4,5},{6,7},{1,0},{3,2},{5,4},{7,6},{8,9},{10,11},{12,... | collective-permute-start | bytes 36872 | tf_op jit(solution)/shard_map/ppermute | solution.py:41
  179.0 3.7 %collective-permute-start.46 = (f32[24,128]{1,0:T(8,128)S(1)}, f32[24,128]{1,0:T(8,128)S(1)}, u32[]{:S(2)}, u32[]{:S(2)}) collective-permute-start(f32[24,128]{1,0:T(8,128)S(1)} %get-tuple-element.73), channel_id=1, source_target_pairs={{0,4},{2,6},{4,0},{6,2},{1,5},{3,7},{5,1},{7,3},{8,12},{10,14},{12... | collective-permute-start | bytes 36872 | tf_op jit(solution)/shard_map/ppermute | solution.py:41
  179.6 4.9 %collective-permute-start.47 = (f32[24,128]{1,0:T(8,128)S(1)}, f32[24,128]{1,0:T(8,128)S(1)}, u32[]{:S(2)}, u32[]{:S(2)}) collective-permute-start(f32[24,128]{1,0:T(8,128)S(1)} %get-tuple-element.73), channel_id=1, source_target_pairs={{0,5},{2,7},{4,1},{6,3},{1,4},{3,6},{5,0},{7,2},{8,13},{10,15},{12... | collective-permute-start | bytes 36872 | tf_op jit(solution)/shard_map/ppermute | solution.py:41
  (31 other events, 179.2 us)
where the time goes:
time: 186 us; the launch traced here: 185 us
  waiting for transfers between devices  77.3 us (42%)
  starting transfers between devices  49.5 us (27%)
  Pallas kernels  37 us (20%)
  local copies, waits for them, and re-layouts  15.2 us (8%)
  other arithmetic  5.47 us (3%)
    ppermute x48, waiting for transfers between devices, send(): return lax.ppermute(value, AXES, moved(masks))  77.3 us
    ppermute x48, starting transfers between devices, send(): return lax.ppermute(value, AXES, moved(masks))  49.5 us
    pallas_call x2, Pallas kernels, screen(): pl.pallas_call(functools.partial(screen_kernel, parts), grid_spec=pltpu.P...  31 us
    unnamed x100, local copies, waits for them, and re-layouts  12.2 us
    pallas_call x1, Pallas kernels, project(): pl.pallas_call(project_kernel, grid_spec=pltpu.PrefetchScalarGridSpec(num...  5.94 us
  transfers between devices with their start and end apart: 48, of which 29 were waited for; matrix products, arithmetic and copies ran while one was open for 5% of the time, Pallas kernels for 17%

commit v1 on v0

--- a/solution.py
+++ b/solution.py
@@ -24,10 +24,8 @@
 SEQ = ("ZYzyx", "ZYyxz", "ZYxzy", "vZYzy")
 HALF = CHIPS // 2
 
-
 def device(y, z, x, core):
     return (((y * NZ + z) * 2 + x % 2) * 2 + core) * 2 + x // 2
-
 
 def moved(masks):
     pairs = []
@@ -36,19 +34,15 @@
         pairs.append((device(y, z, x, core), device(y ^ my, z ^ mz, x ^ mx, core ^ mc)))
     return pairs
 
-
 def send(value, masks):
     return lax.ppermute(value, AXES, moved(masks))
-
 
 def step(value, letter):
     dim, *per_core = STEPS[letter]
     return send(value, [tuple(mask if dim == name else 0 for name in "yzx") + (0,) for mask in per_core])
 
-
 def core_swap(value):
     return send(value, [(0, 0, 0, 1)] * 2)
-
 
 def offsets(seq):
     table = np.zeros((2, CHIPS), np.int32)
@@ -61,12 +55,11 @@
             table[core, place] = off["y"] * 8 + off["z"] * 2 + (off["x"] & 1)
     return table
 
-
 def screen_kernel(parts, rows, *refs):
     count = len(parts)
-    given = [refs[11 * n : 11 * n + 11] for n in range(count)]
-    screening = refs[11 * count : 11 * count + 2]
-    out, mates, weights, dens, slots, msem, wsem, ssem = refs[11 * count + 2 :]
+    given = [refs[8 * n : 8 * n + 8] for n in range(count)]
+    screening = refs[8 * count : 8 * count + 2]
+    out, mates, weights, dens, slots, msem, wsem, ssem = refs[8 * count + 2 :]
     column = pl.multiple_of(rows[192], 128)
 
     def load_slot(slot, cut):
@@ -74,10 +67,12 @@
         return pltpu.make_async_copy(source, slots.at[slot, cut], ssem.at[slot, cut])
 
     def load(n):
-        for source, first, size in zip(given[n], (0, 8, 16, 24, 32, 48, 56), (8, 8, 8, 8, 16, 8, 8)):
-            pltpu.make_async_copy(source, mates.at[n % 2, pl.ds(first, size)], msem.at[n % 2]).start()
-        for k in range(4):
-            pltpu.make_async_copy(given[n][7 + k], weights.at[n % 2, pl.ds(8 * k, 8)], wsem.at[n % 2]).start()
+        for k in range(8):
+            rows_of = pl.ds(8 * k, 8)
+            if k < 4:
+                bands = given[n][k].at[:, pl.ds(16, 16)]
+                pltpu.make_async_copy(bands, weights.at[n % 2, rows_of], wsem.at[n % 2]).start()
+            pltpu.make_async_copy(given[n][k].at[:, pl.ds(0, 16)], mates.at[n % 2, rows_of], msem.at[n % 2]).start()
 
     def loaded(n):
         pltpu.make_async_copy(mates.at[n % 2], mates.at[n % 2], msem.at[n % 2]).wait()
@@ -136,7 +131,6 @@
         if turn % 2 and turn // 2 + 2 < count:
             load(turn // 2 + 2)
 
-
 def screen(parts, rows, sources, wa, wb):
     vmem = pl.BlockSpec(memory_space=pltpu.VMEM)
     anywhere = pl.BlockSpec(memory_space=pl.ANY)
@@ -146,11 +140,11 @@
         grid_spec=pltpu.PrefetchScalarGridSpec(
             num_scalar_prefetch=1,
             grid=(),
-            in_specs=[anywhere] * (11 * count + 2),
+            in_specs=[anywhere] * (8 * count + 2),
             out_specs=vmem,
             scratch_shapes=[
-                pltpu.VMEM((2, 2 * CHIPS, 16, 2048), jnp.bfloat16),
-                pltpu.VMEM((2, CHIPS, 16, 2048), jnp.bfloat16),
+                pltpu.VMEM((min(count, 2), 2 * CHIPS, 16, 2048), jnp.bfloat16),
+                pltpu.VMEM((min(count, 2), CHIPS, 16, 2048), jnp.bfloat16),
                 pltpu.VMEM((2, 2, HALF * 16, 2048), jnp.bfloat16),
                 pltpu.VMEM((2, 4, 2048, 256), jnp.bfloat16),
                 pltpu.SemaphoreType.DMA((2,)),
@@ -159,13 +153,12 @@
             ],
         ),
         out_shape=jax.ShapeDtypeStruct((count, CHIPS, 16, 1024), jnp.float32),
-        compiler_params=pltpu.CompilerParams(vmem_limit_bytes=50 << 20),
+        compiler_params=pltpu.CompilerParams(vmem_limit_bytes=46 << 20),
         cost_estimate=pl.CostEstimate(flops=4_300_000_000 * count, bytes_accessed=8 << 20, transcendentals=0),
     )(rows, *sources, wa, wb)
 
-
-def project_kernel(place, f0, f12, v0, v1, v2, v3, *outs):
-    folded = (f0.at[0], f12.at[0], f12.at[1])
+def project_kernel(place, f0, f21, v0, v1, v2, v3, *outs):
+    folded = (f0.at[0], f21.at[1], f21.at[0])
 
     def pick(where):
         slot, kind = lax.bitwise_and(where, 7), where // 8
@@ -186,7 +179,6 @@
             terms = both[:48] + both[48:]
             outs[group][unit] = jnp.concatenate([terms[:24], terms[24:]], axis=1)
 
-
 def project(place, folded, val):
     vmem = pl.BlockSpec(memory_space=pltpu.VMEM)
     return pl.pallas_call(
@@ -199,7 +191,6 @@
         cost_estimate=pl.CostEstimate(flops=800_000_000, bytes_accessed=10 << 20, transcendentals=0),
     )(place, *folded, *val)
 
-
 def spread(parts, dim, masks):
     moves = []
     for mask in masks:
@@ -207,11 +198,9 @@
         moves.append(send(parts[mask], [one] * 2))
     return (parts[0] + moves[0]) + (moves[1] + moves[2])
 
-
 def lookup(keys, table):
     spots = jnp.arange(table.shape[-1], dtype=jnp.int32)
     return jnp.sum(jnp.where(keys[..., None] == spots, table[..., None, :], 0), axis=-1)
-
 
 def tables(chip, core, pa, pair_transfer, owner_map):
     owned = lax.dynamic_slice_in_dim(owner_map, chip * 2, 2)
@@ -229,7 +218,6 @@
     rows = jnp.concatenate([rows.reshape(-1), (pa * 1024).astype(jnp.int32)[None]])
     return rows, mine(place).reshape(-1)
 
-
 def shards(conduction, weighted, valence, screening, pair_transfer, owner_map):
     ka, pa = lax.axis_index("ka"), lax.axis_index("pa")
     chip, core = ka // 2, ka % 2
@@ -237,42 +225,31 @@
     mine = screening[0]
 
     stream = jnp.concatenate([conduction, weighted], axis=1)
-    val = [valence]
-    for turn in range(2):
-        moves = [step(stream, SEQ[0][turn]), step(val[0], SEQ[3][turn])]
-        stream, val, moves = lax.optimization_barrier((stream, val, moves))
-        stream = jnp.concatenate([stream, moves[0]], axis=0)
-        val = [jnp.concatenate([val[0], moves[1]], axis=0)]
-    parts = [slice(16 * part, 16 * part + 16) for part in range(3)]
-    streams = [jnp.concatenate([stream[:, :48][:, cut], stream[:, 48:][:, cut]], axis=1) for cut in parts]
+    units = [stream, step(stream, "Z"), step(stream, "Y")]
+    units.append(step(units[1], "Y"))
+    val = jnp.concatenate([valence, step(valence, SEQ[3][0])], axis=0)
+    units = lax.optimization_barrier(units)
+    streams = []
+    for part in range(3):
+        cut, low = slice(16 * part, 16 * part + 16), slice(48 + 16 * part, 64 + 16 * part)
+        streams.append(jnp.concatenate([jnp.concatenate([one[:, cut], one[:, low]], axis=1) for one in units], axis=0))
     moves = [step(block, SEQ[k][2]) for k, block in enumerate(streams)]
-    val_move = step(val[0], SEQ[3][2])
+    val_move = step(val, SEQ[3][1])
     streams, moves = lax.optimization_barrier((streams, moves))
-    cond = [[jnp.concatenate([one[:, :16], two[:, :16]], axis=0)] for one, two in zip(streams, moves)]
-    weights = [[jnp.concatenate([one[:, 16:], two[:, 16:]], axis=0)] for one, two in zip(streams, moves)]
-
-    def onward(pieces, source, turn):
+    pieces = [[jnp.concatenate(pair, axis=0)] for pair in zip(streams, moves)]
+    for source, turn in ((0, 3), (0, 4), (1, 4)):
         for k, held in enumerate(pieces):
             held.append(step(held[source], SEQ[k][turn]))
-
-    onward(cond, 0, 3)
-    onward(cond, 0, 4)
-    onward(cond, 1, 4)
-    onward(weights, 0, 3)
-    onward(weights, 0, 4)
-    onward(weights, 1, 4)
-    val = jnp.concatenate([val[0], val_move], axis=0)
+    val = jnp.concatenate([val, val_move], axis=0)
+    val = jnp.concatenate([val, step(val, SEQ[3][2])], axis=0)
     swapped = core_swap(mine)
     val_next, val_far = step(val, SEQ[3][3]), step(val, SEQ[3][4])
-    others = []
-    for held in cond:
-        both = [jnp.concatenate(held[:2], axis=0), held[2], held[3]]
-        others.append([core_swap(block) for block in both])
-    inputs = [held + other + weight for held, other, weight in zip(cond, others, weights)]
-    first = screen((0,), rows, inputs[0], mine, swapped)
-    first, val_next = lax.optimization_barrier((first, val_next))
     val_last = step(val_next, SEQ[3][4])
-    folded = [first, screen((1, 2), rows, inputs[1] + inputs[2], mine, swapped)]
+    inputs = []
+    for held in pieces:
+        inputs.append(held + [core_swap(block) for block in held])
+    folded = [screen((0,), rows, inputs[0], mine, swapped)]
+    folded.append(screen((2, 1), rows, inputs[2] + inputs[1], mine, swapped))
     folded, val_last = lax.optimization_barrier((folded, val_last))
     terms = project(place, folded, (val, val_next, val_far, val_last))
     terms = spread(terms, "y", (1, 3, 2))
@@ -283,7 +260,6 @@
     across = send(terms[0], [(0, 0, 2, 0)] * 2)
     total = (terms[0] + across) + (near + wrap)
     return jnp.concatenate([total[:, :64], total[:, 64:]], axis=0)[None]
-
 
 def solution(mesh):
     in_specs = (

time: 186 us -> 177 us (0.952)
  starting transfers between devices: 49.5 us -> 45 us
  waiting for transfers between devices: 77.3 us -> 79.8 us
  local copies, waits for them, and re-layouts: 15.2 us -> 12.8 us
  Pallas kernels: 37 us -> 34.9 us
  other arithmetic: 5.47 us -> 3.53 us
    ppermute x48 -> x43, starting transfers between devices: 49.5 us -> 45 us  [send(): return lax.ppermute(value, AXES, moved(masks))]
    ppermute x48 -> x43, waiting for transfers between devices: 77.3 us -> 79.8 us  [send(): return lax.ppermute(value, AXES, moved(masks))]
    concatenate x13 -> x5, other arithmetic: 3.94 us -> 2 us  [the longest x1 0.96 us: shards(): val = jnp.concatenate([val, val_move], axis=0)]
    unnamed x100 -> x73, local copies, waits for them, and re-layouts: 12.2 us -> 11.1 us
  transfers between devices with their start and end apart: 48 -> 43, of which waited for: 29 -> 18; matrix products, arithmetic and copies ran while one was open for 5% -> 2% of each run, Pallas kernels for 17% -> 17%
where the time goes in v1:
time: 177 us
  waiting for transfers between devices  79.8 us (45%)
  starting transfers between devices  45 us (25%)
  Pallas kernels  34.9 us (20%)
  local copies, waits for them, and re-layouts  12.8 us (7%)
  other arithmetic  3.53 us (2%)
    ppermute x43, waiting for transfers between devices, send(): return lax.ppermute(value, AXES, moved(masks))  79.8 us
    ppermute x43, starting transfers between devices, send(): return lax.ppermute(value, AXES, moved(masks))  45 us
    pallas_call x2, Pallas kernels, screen(): pl.pallas_call(functools.partial(screen_kernel, parts), grid_spec=pltpu.P...  30.5 us
    unnamed x73, local copies, waits for them, and re-layouts  11.1 us
    pallas_call x1, Pallas kernels, project(): pl.pallas_call(project_kernel, grid_spec=pltpu.PrefetchScalarGridSpec(num...  4.4 us
  transfers between devices with their start and end apart: 43, of which 18 were waited for; matrix products, arithmetic and copies ran while one was open for 2% of the time, Pallas kernels for 17%

profile of v1, /device:TPU:0, one launch (start us, length us, event | category | flops | bytes accessed | tf_op | source)
XLA Modules:
  0.0 176.6 jit_solution(15241358300491438722)
XLA Ops:
  0.0 0.9 constant_dynamic-update-slice_fusion.1
  1.0 1.0 constant_dynamic-update-slice_fusion
  1.9 4.2 %collective-permute-start = (bf16[1,96,2048]{2,1,0:T(8,128)(2,1)S(1)}, bf16[1,96,2048]{2,1,0:T(8,128)(2,1)S(1)}, u32[]{:S(2)}, u32[]{:S(2)}) collective-permute-start(bf16[1,96,2048]{2,1,0:T(8,128)(2,1)S(1)} %constant_dynamic-update-slice_fusion), channel_id=1, source_target_pairs={{0,24},{2,10},{4,28},{6,14},{1,25},{3,11},{5,29},{7,15},{8,16},{10... | collective-permute-start | bytes 1179656 | tf_op jit(solution)/shard_map/ppermute | solution.py:38
  6.2 1.5 collective-permute-start.28
  7.7 3.0 %collective-permute-start.1 = (bf16[1,96,2048]{2,1,0:T(8,128)(2,1)S(1)}, bf16[1,96,2048]{2,1,0:T(8,128)(2,1)S(1)}, u32[]{:S(2)}, u32[]{:S(2)}) collective-permute-start(bf16[1,96,2048]{2,1,0:T(8,128)(2,1)S(1)} %constant_dynamic-update-slice_fusion), channel_id=1, source_target_pairs={{0,96},{2,34},{4,100},{6,38},{1,97},{3,35},{5,101},{7,39},{8,104},... | collective-permute-start | bytes 1179656 | tf_op jit(solution)/shard_map/ppermute | solution.py:38
  10.7 1.2 collective-permute-done
  11.9 3.0 %collective-permute-start.2 = (bf16[1,96,2048]{2,1,0:T(8,128)(2,1)S(1)}, bf16[1,96,2048]{2,1,0:T(8,128)(2,1)S(1)}, u32[]{:S(2)}, u32[]{:S(2)}) collective-permute-start(bf16[1,96,2048]{2,1,0:T(8,128)(2,1)S(1)} %collective-permute-done), channel_id=1, source_target_pairs={{0,96},{2,34},{4,100},{6,38},{1,97},{3,35},{5,101},{7,39},{8,104},... | collective-permute-start | bytes 1179656 | tf_op jit(solution)/shard_map/ppermute | solution.py:38
  14.9 0.9 pad_maximum_fusion.1
  15.9 3.3 %collective-permute-start.29 = (bf16[2,64,1024]{2,1,0:T(8,128)(2,1)S(1)}, bf16[2,64,1024]{2,1,0:T(8,128)(2,1)S(1)}, u32[]{:S(2)}, u32[]{:S(2)}) collective-permute-start(bf16[2,64,1024]{2,1,0:T(8,128)(2,1)S(1)} %pad_maximum_fusion.1), channel_id=1, source_target_pairs={{0,24},{2,10},{4,28},{6,14},{1,25},{3,11},{5,29},{7,15},{8,16},{10... | collective-permute-start | bytes 786440 | tf_op jit(solution)/shard_map/ppermute | solution.py:38
  19.2 4.4 %collective-permute-done.29 = bf16[2,64,1024]{2,1,0:T(8,128)(2,1)S(1)} collective-permute-done((bf16[2,64,1024]{2,1,0:T(8,128)(2,1)S(1)}, bf16[2,64,1024]{2,1,0:T(8,128)(2,1)S(1)}, u32[]{:S(2)}, u32[]{:S(2)}) %collective-permute-start.29) | collective-permute-done | bytes 262176 | tf_op jit(solution)/shard_map/ppermute | solution.py:38
  23.5 1.0 pad_maximum_fusion
  25.0 1.6 collective-permute-start.5
  26.6 0.4 collective-permute-start.4
  27.4 8.7 %collective-permute-done.30 = bf16[4,64,1024]{2,1,0:T(8,128)(2,1)S(1)} collective-permute-done((bf16[4,64,1024]{2,1,0:T(8,128)(2,1)S(1)}, bf16[4,64,1024]{2,1,0:T(8,128)(2,1)S(1)}, u32[]{:S(2)}, u32[]{:S(2)}) %collective-permute-start.30) | collective-permute-done | bytes 524320 | tf_op jit(solution)/shard_map/ppermute | solution.py:38
  36.1 1.8 %collective-permute-start.31 = (bf16[8,64,1024]{2,1,0:T(8,128)(2,1)S(1)}, bf16[8,64,1024]{2,1,0:T(8,128)(2,1)S(1)}, u32[]{:S(2)}, u32[]{:S(2)}) collective-permute-start(bf16[8,64,1024]{2,1,0:T(8,128)(2,1)S(1)} %constant_dynamic-update-slice_fusion.8.v0), channel_id=1, source_target_pairs={{0,8},{2,26},{4,12},{6,30},{1,9},{3,27},{5,13},{7,31},{8,0},{10,18... | collective-permute-start | bytes 3145736 | tf_op jit(solution)/shard_map/ppermute | solution.py:38
  38.1 0.4 collective-permute-start.14
  38.5 0.4 collective-permute-start.21
  39.1 1.9 %collective-permute-start.22 = (bf16[8,32,2048]{2,1,0:T(8,128)(2,1)S(1)}, bf16[8,32,2048]{2,1,0:T(8,128)(2,1)S(1)}, u32[]{:S(2)}, u32[]{:S(2)}) collective-permute-start(bf16[8,32,2048]{2,1,0:T(8,128)(2,1)S(1)} %constant_dynamic-update-slice_fusion.6.refs_8_), channel_id=1, source_target_pairs={{0,8},{2,26},{4,12},{6,30},{1,9},{3,27},{5,13},{7,31},{8,0},{10,18... | collective-permute-start | bytes 3145736 | tf_op jit(solution)/shard_map/ppermute | solution.py:38
  41.0 10.0 %collective-permute-done.31.v1 = bf16[8,64,1024]{2,1,0:T(8,128)(2,1)S(1)} collective-permute-done((bf16[8,64,1024]{2,1,0:T(8,128)(2,1)S(1)}, bf16[8,64,1024]{2,1,0:T(8,128)(2,1)S(1)}, u32[]{:S(2)}, u32[]{:S(2)}) %collective-permute-start.31) | collective-permute-done | bytes 1048608 | tf_op jit(solution)/shard_map/ppermute | solution.py:38
  51.0 11.2 %collective-permute-done.14.refs_1_ = bf16[8,32,2048]{2,1,0:T(8,128)(2,1)S(1)} collective-permute-done((bf16[8,32,2048]{2,1,0:T(8,128)(2,1)S(1)}, bf16[8,32,2048]{2,1,0:T(8,128)(2,1)S(1)}, u32[]{:S(2)}, u32[]{:S(2)}) %collective-permute-start.14) | collective-permute-done | bytes 1048608 | tf_op jit(solution)/shard_map/ppermute | solution.py:38
  62.3 0.5 collective-permute-start.24
  62.9 0.4 collective-permute-start.6
  63.2 10.2 %collective-permute-done.22.refs_10_ = bf16[8,32,2048]{2,1,0:T(8,128)(2,1)S(1)} collective-permute-done((bf16[8,32,2048]{2,1,0:T(8,128)(2,1)S(1)}, bf16[8,32,2048]{2,1,0:T(8,128)(2,1)S(1)}, u32[]{:S(2)}, u32[]{:S(2)}) %collective-permute-start.22) | collective-permute-done | bytes 1048608 | tf_op jit(solution)/shard_map/ppermute | solution.py:38
  73.9 1.1 copy-done.12
  75.3 2.5 %collective-permute-done.6.refs_1_ = bf16[8,32,2048]{2,1,0:T(8,128)(2,1)S(1)} collective-permute-done((bf16[8,32,2048]{2,1,0:T(8,128)(2,1)S(1)}, bf16[8,32,2048]{2,1,0:T(8,128)(2,1)S(1)}, u32[]{:S(2)}, u32[]{:S(2)}) %collective-permute-start.6) | collective-permute-done | bytes 1048608 | tf_op jit(solution)/shard_map/ppermute | solution.py:38
  77.7 1.7 collective-permute-start.23
  79.5 8.9 %collective-permute-done.7.refs_2_ = bf16[8,32,2048]{2,1,0:T(8,128)(2,1)} collective-permute-done((bf16[8,32,2048]{2,1,0:T(8,128)(2,1)S(1)}, bf16[8,32,2048]{2,1,0:T(8,128)(2,1)}, u32[]{:S(2)}, u32[]{:S(2)}) %collective-permute-start.7) | collective-permute-done | bytes 1048608 | tf_op jit(solution)/shard_map/ppermute | solution.py:38
  88.4 1.0 copy-done.2
  89.4 0.5 collective-permute-start.19
  89.9 1.0 copy-done.10
  90.9 0.6 collective-permute-start.8
  91.5 1.3 collective-permute-done.23.refs_11_
  92.8 1.3 collective-permute-start.25
  94.1 1.0 copy-done.16
  95.1 1.0 copy-done.18
  96.2 0.5 collective-permute-start.11
  97.0 8.8 %collective-permute-done.8.refs_3_ = bf16[8,32,2048]{2,1,0:T(8,128)(2,1)} collective-permute-done((bf16[8,32,2048]{2,1,0:T(8,128)(2,1)S(1)}, bf16[8,32,2048]{2,1,0:T(8,128)(2,1)}, u32[]{:S(2)}, u32[]{:S(2)}) %collective-permute-start.8) | collective-permute-done | bytes 1048608 | tf_op jit(solution)/shard_map/ppermute | solution.py:38
  106.3 0.5 collective-permute-start.26
  107.0 0.4 collective-permute-start.27
  108.2 0.6 collective-permute-done.12.refs_7_
  108.8 1.2 collective-permute-start.32
  110.0 1.2 copy-done.3
  111.2 12.8 %shard_map.118.f0 = f32[1,32,16,1024]{3,2,1,0:T(8,128)} custom-call(s32[193]{0:T(256)S(1)} %pad_add_fusion.rows, bf16[8,32,2048]{2,1,0:T(8,128)(2,1)S(1)} %constant_dynamic-update-slice_fusion.2.refs_0_, bf16[8,32,2048]{2,1,0:T(8,128)(2,1)S(1)} %collective-permute-done.6.refs_1_, bf16[8,32,2048]{2,1,0:T(8,128)(2,1)} %collective-permute-done.7.refs_2_, ...), custom_call_target="tpu_custom_call" | custom-call | flops 4300000256 | bytes 8388608 | tf_op jit(solution)/shard_map/pallas_call | solution.py:138
  124.1 1.4 copy-done.11
  125.5 17.8 %shard_map.119.f21 = f32[2,32,16,1024]{3,2,1,0:T(8,128)} custom-call(s32[193]{0:T(256)S(1)} %pad_add_fusion.rows, bf16[8,32,2048]{2,1,0:T(8,128)(2,1)S(1)} %copy-done.7, bf16[8,32,2048]{2,1,0:T(8,128)(2,1)S(1)} %copy-done.9, bf16[8,32,2048]{2,1,0:T(8,128)(2,1)S(1)} %copy-done.11, bf16[8,32,2048]{2,1,0:T(8,128)(2,1)S(1)} %copy-done.15, ...), custom_call_target="tpu_custom_call" | custom-call | flops 8600000512 | bytes 8388608 | tf_op jit(solution)/shard_map/pallas_call | solution.py:138
  143.3 2.2 %copy-done.1 = f32[2,32,16,1024]{3,2,1,0:T(8,128)S(1)} copy-done((f32[2,32,16,1024]{3,2,1,0:T(8,128)S(1)}, f32[2,32,16,1024]{3,2,1,0:T(8,128)}, u32[]{:S(2)}) %copy-start.1) | copy-done | bytes 4194328
  145.5 4.4 %shard_map.120 = (f32[8,24,128]{2,1,0:T(8,128)S(1)}, f32[8,24,128]{2,1,0:T(8,128)S(1)}, f32[8,24,128]{2,1,0:T(8,128)S(1)}, f32[8,24,128]{2,1,0:T(8,128)S(1)}) custom-call(s32[128]{0:T(128)S(1)} %reshape.27.place, f32[1,32,16,1024]{3,2,1,0:T(8,128)S(1)} %copy-done, f32[2,32,16,1024]{3,2,1,0:T(8,128)S(1)} %copy-done.1, ...), custom_call_target="tpu_custom_call" | custom-call | flops 800000000 | bytes 10485760 | tf_op jit(solution)/shard_map/pallas_call | solution.py:184
  149.9 0.9 collective-permute-start.34
  150.8 2.9 %collective-permute-start.35 = (f32[8,24,128]{2,1,0:T(8,128)S(1)}, f32[8,24,128]{2,1,0:T(8,128)S(1)}, u32[]{:S(2)}, u32[]{:S(2)}) collective-permute-start(f32[8,24,128]{2,1,0:T(8,128)S(1)} %get-tuple-element.37), channel_id=1, source_target_pairs={{0,96},{2,98},{4,100},{6,102},{1,97},{3,99},{5,101},{7,103},{8,104... | collective-permute-start | bytes 294920 | tf_op jit(solution)/shard_map/ppermute | solution.py:38
  153.7 0.6 collective-permute-start.36
  154.3 0.6 collective-permute-done.34
  154.9 3.2 %collective-permute-done.35 = f32[8,24,128]{2,1,0:T(8,128)S(1)} collective-permute-done((f32[8,24,128]{2,1,0:T(8,128)S(1)}, f32[8,24,128]{2,1,0:T(8,128)S(1)}, u32[]{:S(2)}, u32[]{:S(2)}) %collective-permute-start.35) | collective-permute-done | bytes 98336 | tf_op jit(solution)/shard_map/ppermute | solution.py:38
  158.1 1.8 %collective-permute-done.36 = f32[8,24,128]{2,1,0:T(8,128)S(1)} collective-permute-done((f32[8,24,128]{2,1,0:T(8,128)S(1)}, f32[8,24,128]{2,1,0:T(8,128)S(1)}, u32[]{:S(2)}, u32[]{:S(2)}) %collective-permute-start.36) | collective-permute-done | bytes 98336 | tf_op jit(solution)/shard_map/ppermute | solution.py:38
  159.9 0.9 collective-permute-start.37
  160.8 3.1 %collective-permute-start.38 = (f32[2,24,128]{2,1,0:T(8,128)S(1)}, f32[2,24,128]{2,1,0:T(8,128)S(1)}, u32[]{:S(2)}, u32[]{:S(2)}) collective-permute-start(f32[2,24,128]{2,1,0:T(8,128)S(1)} %get-tuple-element.64), channel_id=1, source_target_pairs={{0,24},{2,26},{4,28},{6,30},{1,25},{3,27},{5,29},{7,31},{8,16},{10... | collective-permute-start | bytes 73736 | tf_op jit(solution)/shard_map/ppermute | solution.py:38
  164.0 1.4 collective-permute-start.39
  165.3 0.5 collective-permute-done.38
  165.9 3.4 %collective-permute-done.39 = f32[2,24,128]{2,1,0:T(8,128)S(1)} collective-permute-done((f32[2,24,128]{2,1,0:T(8,128)S(1)}, f32[2,24,128]{2,1,0:T(8,128)S(1)}, u32[]{:S(2)}, u32[]{:S(2)}) %collective-permute-start.39) | collective-permute-done | bytes 24608 | tf_op jit(solution)/shard_map/ppermute | solution.py:38
  169.3 1.2 collective-permute-start.40
  170.5 0.5 collective-permute-start.41
  171.0 2.5 %collective-permute-start.42 = (f32[24,128]{1,0:T(8,128)S(1)}, f32[24,128]{1,0:T(8,128)S(1)}, u32[]{:S(2)}, u32[]{:S(2)}) collective-permute-start(f32[24,128]{1,0:T(8,128)S(1)} %get-tuple-element.67), channel_id=1, source_target_pairs={{0,5},{2,7},{4,1},{6,3},{1,4},{3,6},{5,0},{7,2},{8,13},{10,15},{12... | collective-permute-start | bytes 36872 | tf_op jit(solution)/shard_map/ppermute | solution.py:38
  173.5 1.1 collective-permute-done.40
  174.6 1.3 collective-permute-done.42
  176.0 0.6 maximum_bitcast_fusion
  (130 shorter events, 3.9 us)
Async XLA Ops:
  0.9 26.3 %copy-start.20 = (bf16[1,64,1024]{2,1,0:T(8,128)(2,1)S(1)}, bf16[1,64,1024]{2,1,0:T(8,128)(2,1)}, u32[]{:S(2)}) copy-start(bf16[1,64,1024]{2,1,0:T(8,128)(2,1)} %param.14) | copy-start | bytes 393220
  1.9 10.0 %collective-permute-start = (bf16[1,96,2048]{2,1,0:T(8,128)(2,1)S(1)}, bf16[1,96,2048]{2,1,0:T(8,128)(2,1)S(1)}, u32[]{:S(2)}, u32[]{:S(2)}) collective-permute-start(bf16[1,96,2048]{2,1,0:T(8,128)(2,1)S(1)} %constant_dynamic-update-slice_fusion), channel_id=1, source_target_pairs={{0,24},{2,10},{4,28},{6,14},{1,25},{3,11},{5,29},{7,15},{8,16},{10... | collective-permute-start | bytes 1179656 | tf_op jit(solution)/shard_map/ppermute | solution.py:38
  6.2 8.8 %collective-permute-start.28 = (bf16[1,64,1024]{2,1,0:T(8,128)(2,1)}, bf16[1,64,1024]{2,1,0:T(8,128)(2,1)S(1)}, u32[]{:S(2)}, u32[]{:S(2)}) collective-permute-start(bf16[1,64,1024]{2,1,0:T(8,128)(2,1)} %param.14), channel_id=1, source_target_pairs={{0,4},{2,6},{4,0},{6,2},{1,5},{3,7},{5,1},{7,3},{8,12},{10,14},{12... | collective-permute-start | bytes 393224 | tf_op jit(solution)/shard_map/ppermute | solution.py:38
  7.7 17.1 %collective-permute-start.1 = (bf16[1,96,2048]{2,1,0:T(8,128)(2,1)S(1)}, bf16[1,96,2048]{2,1,0:T(8,128)(2,1)S(1)}, u32[]{:S(2)}, u32[]{:S(2)}) collective-permute-start(bf16[1,96,2048]{2,1,0:T(8,128)(2,1)S(1)} %constant_dynamic-update-slice_fusion), channel_id=1, source_target_pairs={{0,96},{2,34},{4,100},{6,38},{1,97},{3,35},{5,101},{7,39},{8,104},... | collective-permute-start | bytes 1179656 | tf_op jit(solution)/shard_map/ppermute | solution.py:38
  11.9 12.9 %collective-permute-start.2 = (bf16[1,96,2048]{2,1,0:T(8,128)(2,1)S(1)}, bf16[1,96,2048]{2,1,0:T(8,128)(2,1)S(1)}, u32[]{:S(2)}, u32[]{:S(2)}) collective-permute-start(bf16[1,96,2048]{2,1,0:T(8,128)(2,1)S(1)} %collective-permute-done), channel_id=1, source_target_pairs={{0,96},{2,34},{4,100},{6,38},{1,97},{3,35},{5,101},{7,39},{8,104},... | collective-permute-start | bytes 1179656 | tf_op jit(solution)/shard_map/ppermute | solution.py:38
  15.9 7.7 %collective-permute-start.29 = (bf16[2,64,1024]{2,1,0:T(8,128)(2,1)S(1)}, bf16[2,64,1024]{2,1,0:T(8,128)(2,1)S(1)}, u32[]{:S(2)}, u32[]{:S(2)}) collective-permute-start(bf16[2,64,1024]{2,1,0:T(8,128)(2,1)S(1)} %pad_maximum_fusion.1), channel_id=1, source_target_pairs={{0,24},{2,10},{4,28},{6,14},{1,25},{3,11},{5,29},{7,15},{8,16},{10... | collective-permute-start | bytes 786440 | tf_op jit(solution)/shard_map/ppermute | solution.py:38
  24.5 11.6 %collective-permute-start.30 = (bf16[4,64,1024]{2,1,0:T(8,128)(2,1)S(1)}, bf16[4,64,1024]{2,1,0:T(8,128)(2,1)S(1)}, u32[]{:S(2)}, u32[]{:S(2)}) collective-permute-start(bf16[4,64,1024]{2,1,0:T(8,128)(2,1)S(1)} %pad_maximum_fusion), channel_id=1, source_target_pairs={{0,96},{2,34},{4,100},{6,38},{1,97},{3,35},{5,101},{7,39},{8,104},... | collective-permute-start | bytes 1572872 | tf_op jit(solution)/shard_map/ppermute | solution.py:38
  25.0 12.9 %collective-permute-start.5 = (bf16[4,32,2048]{2,1,0:T(8,128)(2,1)S(1)}, bf16[4,32,2048]{2,1,0:T(8,128)(2,1)S(1)}, u32[]{:S(2)}, u32[]{:S(2)}) collective-permute-start(bf16[4,32,2048]{2,1,0:T(8,128)(2,1)S(1)} %maximum_maximum_fusion.2), channel_id=1, source_target_pairs={{0,4},{2,7},{4,0},{6,3},{1,5},{3,6},{5,1},{7,2},{8,12},{10,15},{12... | collective-permute-start | bytes 1572872 | tf_op jit(solution)/shard_map/ppermute | solution.py:38
  26.6 11.3 %collective-permute-start.4 = (bf16[4,32,2048]{2,1,0:T(8,128)(2,1)S(1)}, bf16[4,32,2048]{2,1,0:T(8,128)(2,1)S(1)}, u32[]{:S(2)}, u32[]{:S(2)}) collective-permute-start(bf16[4,32,2048]{2,1,0:T(8,128)(2,1)S(1)} %maximum_maximum_fusion.1), channel_id=1, source_target_pairs={{0,32},{2,98},{4,36},{6,102},{1,33},{3,99},{5,37},{7,103},{8,40},{... | collective-permute-start | bytes 1572872 | tf_op jit(solution)/shard_map/ppermute | solution.py:38
  27.1 69.6 %copy-start.29 = (s32[64]{0:T(128)S(1)}, s32[64]{0:T(128)}, u32[]{:S(2)}) copy-start(s32[64]{0:T(128)} %param.17) | copy-start | bytes 772
  27.1 69.8 %copy-start.27 = (s32[3,32]{1,0:T(4,128)S(1)}, s32[3,32]{1,0:T(4,128)}, u32[]{:S(2)}) copy-start(s32[3,32]{1,0:T(4,128)} %constant.53.clone) | copy-start | bytes 1156
  27.1 69.8 %copy-start.28 = (s32[3,32]{1,0:T(4,128)S(1)}, s32[3,32]{1,0:T(4,128)}, u32[]{:S(2)}) copy-start(s32[3,32]{1,0:T(4,128)} %constant.54.clone) | copy-start | bytes 1156
  27.1 78.7 %copy-start.22 = (s32[64,64]{1,0:T(8,128)S(1)}, s32[64,64]{1,0:T(8,128)}, u32[]{:S(2)}) copy-start(s32[64,64]{1,0:T(8,128)} %param.16) | copy-start | bytes 49156
  27.2 80.2 %copy-start.25 = (s32[3,64]{1,0:T(4,128)S(1)}, s32[3,64]{1,0:T(4,128)}, u32[]{:S(2)}) copy-start(s32[3,64]{1,0:T(4,128)} %constant.55.clone) | copy-start | bytes 2308
  27.2 80.2 %copy-start.26 = (s32[3,64]{1,0:T(4,128)S(1)}, s32[3,64]{1,0:T(4,128)}, u32[]{:S(2)}) copy-start(s32[3,64]{1,0:T(4,128)} %constant.56.clone) | copy-start | bytes 2308
  27.2 10.8 %collective-permute-start.3 = (bf16[4,32,2048]{2,1,0:T(8,128)(2,1)S(1)}, bf16[4,32,2048]{2,1,0:T(8,128)(2,1)S(1)}, u32[]{:S(2)}, u32[]{:S(2)}) collective-permute-start(bf16[4,32,2048]{2,1,0:T(8,128)(2,1)S(1)} %maximum_maximum_fusion), channel_id=1, source_target_pairs={{0,8},{2,26},{4,12},{6,30},{1,9},{3,27},{5,13},{7,31},{8,0},{10,18... | collective-permute-start | bytes 1572872 | tf_op jit(solution)/shard_map/ppermute | solution.py:38
  27.3 80.4 %copy-start.23 = (s32[4,32]{1,0:T(4,128)S(1)}, s32[4,32]{1,0:T(4,128)}, u32[]{:S(2)}) copy-start(s32[4,32]{1,0:T(4,128)} %constant.57.clone) | copy-start | bytes 1540
  27.3 80.4 %copy-start.24 = (s32[4,32]{1,0:T(4,128)S(1)}, s32[4,32]{1,0:T(4,128)}, u32[]{:S(2)}) copy-start(s32[4,32]{1,0:T(4,128)} %constant.58.clone) | copy-start | bytes 1540
  36.1 14.9 %collective-permute-start.31 = (bf16[8,64,1024]{2,1,0:T(8,128)(2,1)S(1)}, bf16[8,64,1024]{2,1,0:T(8,128)(2,1)S(1)}, u32[]{:S(2)}, u32[]{:S(2)}) collective-permute-start(bf16[8,64,1024]{2,1,0:T(8,128)(2,1)S(1)} %constant_dynamic-update-slice_fusion.8.v0), channel_id=1, source_target_pairs={{0,8},{2,26},{4,12},{6,30},{1,9},{3,27},{5,13},{7,31},{8,0},{10,18... | collective-permute-start | bytes 3145736 | tf_op jit(solution)/shard_map/ppermute | solution.py:38
  38.1 56.0 %copy-start.6 = (bf16[8,32,2048]{2,1,0:T(8,128)(2,1)}, bf16[8,32,2048]{2,1,0:T(8,128)(2,1)S(1)}, u32[]{:S(2)}) copy-start(bf16[8,32,2048]{2,1,0:T(8,128)(2,1)S(1)} %constant_dynamic-update-slice_fusion.4.refs_0_) | copy-start | bytes 3145732
  38.1 24.2 %collective-permute-start.14 = (bf16[8,32,2048]{2,1,0:T(8,128)(2,1)S(1)}, bf16[8,32,2048]{2,1,0:T(8,128)(2,1)S(1)}, u32[]{:S(2)}, u32[]{:S(2)}) collective-permute-start(bf16[8,32,2048]{2,1,0:T(8,128)(2,1)S(1)} %constant_dynamic-update-slice_fusion.4.refs_0_), channel_id=1, source_target_pairs={{0,8},{2,26},{4,12},{6,30},{1,9},{3,27},{5,13},{7,31},{8,0},{10,18... | collective-permute-start | bytes 3145736 | tf_op jit(solution)/shard_map/ppermute | solution.py:38
  38.5 58.1 %copy-start.21 = (bf16[8,32,2048]{2,1,0:T(8,128)(2,1)}, bf16[8,32,2048]{2,1,0:T(8,128)(2,1)S(1)}, u32[]{:S(2)}) copy-start(bf16[8,32,2048]{2,1,0:T(8,128)(2,1)S(1)} %constant_dynamic-update-slice_fusion.6.refs_8_) | copy-start | bytes 3145732
  38.5 23.7 %collective-permute-start.21 = (bf16[8,32,2048]{2,1,0:T(8,128)(2,1)S(1)}, bf16[8,32,2048]{2,1,0:T(8,128)(2,1)}, u32[]{:S(2)}, u32[]{:S(2)}) collective-permute-start(bf16[8,32,2048]{2,1,0:T(8,128)(2,1)S(1)} %constant_dynamic-update-slice_fusion.6.refs_8_), channel_id=1, source_target_pairs={{0,4},{2,7},{4,0},{6,3},{1,5},{3,6},{5,1},{7,2},{8,12},{10,15},{12... | collective-permute-start | bytes 3145736 | tf_op jit(solution)/shard_map/ppermute | solution.py:38
  39.0 23.9 %collective-permute-start.15 = (bf16[8,32,2048]{2,1,0:T(8,128)(2,1)S(1)}, bf16[8,32,2048]{2,1,0:T(8,128)(2,1)S(1)}, u32[]{:S(2)}, u32[]{:S(2)}) collective-permute-start(bf16[8,32,2048]{2,1,0:T(8,128)(2,1)S(1)} %constant_dynamic-update-slice_fusion.4.refs_0_), channel_id=1, source_target_pairs={{0,32},{2,98},{4,36},{6,102},{1,33},{3,99},{5,37},{7,103},{8,40},{... | collective-permute-start | bytes 3145736 | tf_op jit(solution)/shard_map/ppermute | solution.py:38
  39.1 34.3 %collective-permute-start.22 = (bf16[8,32,2048]{2,1,0:T(8,128)(2,1)S(1)}, bf16[8,32,2048]{2,1,0:T(8,128)(2,1)S(1)}, u32[]{:S(2)}, u32[]{:S(2)}) collective-permute-start(bf16[8,32,2048]{2,1,0:T(8,128)(2,1)S(1)} %constant_dynamic-update-slice_fusion.6.refs_8_), channel_id=1, source_target_pairs={{0,8},{2,26},{4,12},{6,30},{1,9},{3,27},{5,13},{7,31},{8,0},{10,18... | collective-permute-start | bytes 3145736 | tf_op jit(solution)/shard_map/ppermute | solution.py:38
  51.0 43.0 %copy-start.4 = (bf16[8,64,1024]{2,1,0:T(8,128)(2,1)}, bf16[8,64,1024]{2,1,0:T(8,128)(2,1)S(1)}, u32[]{:S(2)}) copy-start(bf16[8,64,1024]{2,1,0:T(8,128)(2,1)S(1)} %collective-permute-done.31.v1) | copy-start | bytes 3145732
  51.0 22.8 %collective-permute-start.17 = (bf16[8,32,2048]{2,1,0:T(8,128)(2,1)S(1)}, bf16[8,32,2048]{2,1,0:T(8,128)(2,1)S(1)}, u32[]{:S(2)}, u32[]{:S(2)}) collective-permute-start(bf16[8,32,2048]{2,1,0:T(8,128)(2,1)S(1)} %constant_dynamic-update-slice_fusion.4.refs_0_), channel_id=1, source_target_pairs={{0,2},{2,0},{4,6},{6,4},{1,3},{3,1},{5,7},{7,5},{8,10},{10,8},{12,... | collective-permute-start | bytes 3145736 | tf_op jit(solution)/shard_map/ppermute | solution.py:38
  62.2 32.9 %copy-start.8 = (bf16[8,32,2048]{2,1,0:T(8,128)(2,1)}, bf16[8,32,2048]{2,1,0:T(8,128)(2,1)S(1)}, u32[]{:S(2)}) copy-start(bf16[8,32,2048]{2,1,0:T(8,128)(2,1)S(1)} %collective-permute-done.14.refs_1_) | copy-start | bytes 3145732
  62.3 45.7 %collective-permute-start.13 = (bf16[2048,1024]{1,0:T(8,128)(2,1)}, bf16[2048,1024]{1,0:T(8,128)(2,1)}, u32[]{:S(2)}, u32[]{:S(2)}) collective-permute-start(bf16[2048,1024]{1,0:T(8,128)(2,1)} %bitcast.1.refs_8_.refs_16_), channel_id=1, source_target_pairs={{0,2},{2,0},{4,6},{6,4},{1,3},{3,1},{5,7},{7,5},{8,10},{10,8},{12,... | collective-permute-start | bytes 12582920 | tf_op jit(solution)/shard_map/ppermute | solution.py:38
  62.3 12.7 %collective-permute-start.24 = (bf16[8,32,2048]{2,1,0:T(8,128)(2,1)S(1)}, bf16[8,32,2048]{2,1,0:T(8,128)(2,1)S(1)}, u32[]{:S(2)}, u32[]{:S(2)}) collective-permute-start(bf16[8,32,2048]{2,1,0:T(8,128)(2,1)S(1)} %constant_dynamic-update-slice_fusion.6.refs_8_), channel_id=1, source_target_pairs={{0,2},{2,0},{4,6},{6,4},{1,3},{3,1},{5,7},{7,5},{8,10},{10,8},{12,... | collective-permute-start | bytes 3145736 | tf_op jit(solution)/shard_map/ppermute | solution.py:38
  62.9 14.9 %collective-permute-start.6 = (bf16[8,32,2048]{2,1,0:T(8,128)(2,1)S(1)}, bf16[8,32,2048]{2,1,0:T(8,128)(2,1)S(1)}, u32[]{:S(2)}, u32[]{:S(2)}) collective-permute-start(bf16[8,32,2048]{2,1,0:T(8,128)(2,1)S(1)} %constant_dynamic-update-slice_fusion.2.refs_0_), channel_id=1, source_target_pairs={{0,32},{2,98},{4,36},{6,102},{1,33},{3,99},{5,37},{7,103},{8,40},{... | collective-permute-start | bytes 3145736 | tf_op jit(solution)/shard_map/ppermute | solution.py:38
  73.5 23.2 %copy-start.30 = (bf16[8,32,2048]{2,1,0:T(8,128)(2,1)}, bf16[8,32,2048]{2,1,0:T(8,128)(2,1)S(1)}, u32[]{:S(2)}) copy-start(bf16[8,32,2048]{2,1,0:T(8,128)(2,1)S(1)} %collective-permute-done.22.refs_10_) | copy-start | bytes 3145732
  73.5 14.9 %collective-permute-start.7 = (bf16[8,32,2048]{2,1,0:T(8,128)(2,1)S(1)}, bf16[8,32,2048]{2,1,0:T(8,128)(2,1)}, u32[]{:S(2)}, u32[]{:S(2)}) collective-permute-start(bf16[8,32,2048]{2,1,0:T(8,128)(2,1)S(1)} %constant_dynamic-update-slice_fusion.2.refs_0_), channel_id=1, source_target_pairs={{0,4},{2,7},{4,0},{6,3},{1,5},{3,6},{5,1},{7,2},{8,12},{10,15},{12... | collective-permute-start | bytes 3145736 | tf_op jit(solution)/shard_map/ppermute | solution.py:38
  74.9 13.5 %collective-permute-start.9 = (bf16[8,32,2048]{2,1,0:T(8,128)(2,1)S(1)}, bf16[8,32,2048]{2,1,0:T(8,128)(2,1)S(1)}, u32[]{:S(2)}, u32[]{:S(2)}) collective-permute-start(bf16[8,32,2048]{2,1,0:T(8,128)(2,1)S(1)} %constant_dynamic-update-slice_fusion.2.refs_0_), channel_id=1, source_target_pairs={{0,2},{2,0},{4,6},{6,4},{1,3},{3,1},{5,7},{7,5},{8,10},{10,8},{12,... | collective-permute-start | bytes 3145736 | tf_op jit(solution)/shard_map/ppermute | solution.py:38
  74.9 21.7 %copy-start.31 = (bf16[8,32,2048]{2,1,0:T(8,128)(2,1)}, bf16[8,32,2048]{2,1,0:T(8,128)(2,1)S(1)}, u32[]{:S(2)}) copy-start(bf16[8,32,2048]{2,1,0:T(8,128)(2,1)S(1)} %collective-permute-done.24.refs_12_) | copy-start | bytes 3145732
  74.9 16.0 %collective-permute-start.16 = (bf16[8,32,2048]{2,1,0:T(8,128)(2,1)S(1)}, bf16[8,32,2048]{2,1,0:T(8,128)(2,1)S(1)}, u32[]{:S(2)}, u32[]{:S(2)}) collective-permute-start(bf16[8,32,2048]{2,1,0:T(8,128)(2,1)S(1)} %collective-permute-done.14.refs_1_), channel_id=1, source_target_pairs={{0,32},{2,98},{4,36},{6,102},{1,33},{3,99},{5,37},{7,103},{8,40},{... | collective-permute-start | bytes 3145736 | tf_op jit(solution)/shard_map/ppermute | solution.py:38
  77.7 15.0 %collective-permute-start.23 = (bf16[8,32,2048]{2,1,0:T(8,128)(2,1)}, bf16[8,32,2048]{2,1,0:T(8,128)(2,1)S(1)}, u32[]{:S(2)}, u32[]{:S(2)}) collective-permute-start(bf16[8,32,2048]{2,1,0:T(8,128)(2,1)} %collective-permute-done.21.refs_9_), channel_id=1, source_target_pairs={{0,8},{2,26},{4,12},{6,30},{1,9},{3,27},{5,13},{7,31},{8,0},{10,18... | collective-permute-start | bytes 3145736 | tf_op jit(solution)/shard_map/ppermute | solution.py:38
  88.4 5.7 %collective-permute-start.18 = (bf16[8,32,2048]{2,1,0:T(8,128)(2,1)S(1)}, bf16[8,32,2048]{2,1,0:T(8,128)(2,1)S(1)}, u32[]{:S(2)}, u32[]{:S(2)}) collective-permute-start(bf16[8,32,2048]{2,1,0:T(8,128)(2,1)S(1)} %collective-permute-done.14.refs_1_), channel_id=1, source_target_pairs={{0,2},{2,0},{4,6},{6,4},{1,3},{3,1},{5,7},{7,5},{8,10},{10,8},{12,... | collective-permute-start | bytes 3145736 | tf_op jit(solution)/shard_map/ppermute | solution.py:38
  89.4 5.8 %collective-permute-start.19 = (bf16[8,32,2048]{2,1,0:T(8,128)(2,1)S(1)}, bf16[8,32,2048]{2,1,0:T(8,128)(2,1)S(1)}, u32[]{:S(2)}, u32[]{:S(2)}) collective-permute-start(bf16[8,32,2048]{2,1,0:T(8,128)(2,1)S(1)} %collective-permute-done.15.refs_2_), channel_id=1, source_target_pairs={{0,2},{2,0},{4,6},{6,4},{1,3},{3,1},{5,7},{7,5},{8,10},{10,8},{12,... | collective-permute-start | bytes 3145736 | tf_op jit(solution)/shard_map/ppermute | solution.py:38
  90.9 14.9 %collective-permute-start.8 = (bf16[8,32,2048]{2,1,0:T(8,128)(2,1)S(1)}, bf16[8,32,2048]{2,1,0:T(8,128)(2,1)}, u32[]{:S(2)}, u32[]{:S(2)}) collective-permute-start(bf16[8,32,2048]{2,1,0:T(8,128)(2,1)S(1)} %collective-permute-done.6.refs_1_), channel_id=1, source_target_pairs={{0,4},{2,7},{4,0},{6,3},{1,5},{3,6},{5,1},{7,2},{8,12},{10,15},{12... | collective-permute-start | bytes 3145736 | tf_op jit(solution)/shard_map/ppermute | solution.py:38
  92.8 13.6 %collective-permute-start.25 = (bf16[8,32,2048]{2,1,0:T(8,128)(2,1)}, bf16[8,32,2048]{2,1,0:T(8,128)(2,1)}, u32[]{:S(2)}, u32[]{:S(2)}) collective-permute-start(bf16[8,32,2048]{2,1,0:T(8,128)(2,1)} %collective-permute-done.21.refs_9_), channel_id=1, source_target_pairs={{0,2},{2,0},{4,6},{6,4},{1,3},{3,1},{5,7},{7,5},{8,10},{10,8},{12,... | collective-permute-start | bytes 3145736 | tf_op jit(solution)/shard_map/ppermute | solution.py:38
  95.1 11.8 %collective-permute-start.10 = (bf16[8,32,2048]{2,1,0:T(8,128)(2,1)S(1)}, bf16[8,32,2048]{2,1,0:T(8,128)(2,1)}, u32[]{:S(2)}, u32[]{:S(2)}) collective-permute-start(bf16[8,32,2048]{2,1,0:T(8,128)(2,1)S(1)} %collective-permute-done.6.refs_1_), channel_id=1, source_target_pairs={{0,2},{2,0},{4,6},{6,4},{1,3},{3,1},{5,7},{7,5},{8,10},{10,8},{12,... | collective-permute-start | bytes 3145736 | tf_op jit(solution)/shard_map/ppermute | solution.py:38
  96.2 10.8 %collective-permute-start.11 = (bf16[8,32,2048]{2,1,0:T(8,128)(2,1)}, bf16[8,32,2048]{2,1,0:T(8,128)(2,1)}, u32[]{:S(2)}, u32[]{:S(2)}) collective-permute-start(bf16[8,32,2048]{2,1,0:T(8,128)(2,1)} %collective-permute-done.7.refs_2_), channel_id=1, source_target_pairs={{0,2},{2,0},{4,6},{6,4},{1,3},{3,1},{5,7},{7,5},{8,10},{10,8},{12,... | collective-permute-start | bytes 3145736 | tf_op jit(solution)/shard_map/ppermute | solution.py:38
  105.8 3.0 %collective-permute-start.12 = (bf16[8,32,2048]{2,1,0:T(8,128)(2,1)}, bf16[8,32,2048]{2,1,0:T(8,128)(2,1)}, u32[]{:S(2)}, u32[]{:S(2)}) collective-permute-start(bf16[8,32,2048]{2,1,0:T(8,128)(2,1)} %collective-permute-done.8.refs_3_), channel_id=1, source_target_pairs={{0,2},{2,0},{4,6},{6,4},{1,3},{3,1},{5,7},{7,5},{8,10},{10,8},{12,... | collective-permute-start | bytes 3145736 | tf_op jit(solution)/shard_map/ppermute | solution.py:38
  106.3 17.7 %collective-permute-start.26 = (bf16[8,32,2048]{2,1,0:T(8,128)(2,1)}, bf16[8,32,2048]{2,1,0:T(8,128)(2,1)}, u32[]{:S(2)}, u32[]{:S(2)}) collective-permute-start(bf16[8,32,2048]{2,1,0:T(8,128)(2,1)} %copy-done.30), channel_id=1, source_target_pairs={{0,2},{2,0},{4,6},{6,4},{1,3},{3,1},{5,7},{7,5},{8,10},{10,8},{12,... | collective-permute-start | bytes 3145736 | tf_op jit(solution)/shard_map/ppermute | solution.py:38
  106.8 17.2 %collective-permute-start.20 = (bf16[8,32,2048]{2,1,0:T(8,128)(2,1)}, bf16[8,32,2048]{2,1,0:T(8,128)(2,1)}, u32[]{:S(2)}, u32[]{:S(2)}) collective-permute-start(bf16[8,32,2048]{2,1,0:T(8,128)(2,1)} %copy-done.14), channel_id=1, source_target_pairs={{0,2},{2,0},{4,6},{6,4},{1,3},{3,1},{5,7},{7,5},{8,10},{10,8},{12,... | collective-permute-start | bytes 3145736 | tf_op jit(solution)/shard_map/ppermute | solution.py:38
  107.0 17.1 %collective-permute-start.27 = (bf16[8,32,2048]{2,1,0:T(8,128)(2,1)}, bf16[8,32,2048]{2,1,0:T(8,128)(2,1)}, u32[]{:S(2)}, u32[]{:S(2)}) collective-permute-start(bf16[8,32,2048]{2,1,0:T(8,128)(2,1)} %copy-done.32), channel_id=1, source_target_pairs={{0,2},{2,0},{4,6},{6,4},{1,3},{3,1},{5,7},{7,5},{8,10},{10,8},{12,... | collective-permute-start | bytes 3145736 | tf_op jit(solution)/shard_map/ppermute | solution.py:38
  107.9 35.3 %collective-permute-start.33 = (bf16[8,64,1024]{2,1,0:T(8,128)(2,1)S(1)}, bf16[8,64,1024]{2,1,0:T(8,128)(2,1)S(1)}, u32[]{:S(2)}, u32[]{:S(2)}) collective-permute-start(bf16[8,64,1024]{2,1,0:T(8,128)(2,1)S(1)} %constant_dynamic-update-slice_fusion.8.v0), channel_id=1, source_target_pairs={{0,32},{2,98},{4,36},{6,102},{1,33},{3,99},{5,37},{7,103},{8,40},{... | collective-permute-start | bytes 3145736 | tf_op jit(solution)/shard_map/ppermute | solution.py:38
  108.8 34.5 %collective-permute-start.32 = (bf16[8,64,1024]{2,1,0:T(8,128)(2,1)}, bf16[8,64,1024]{2,1,0:T(8,128)(2,1)S(1)}, u32[]{:S(2)}, u32[]{:S(2)}) collective-permute-start(bf16[8,64,1024]{2,1,0:T(8,128)(2,1)} %copy-done.4), channel_id=1, source_target_pairs={{0,32},{2,98},{4,36},{6,102},{1,33},{3,99},{5,37},{7,103},{8,40},{... | collective-permute-start | bytes 3145736 | tf_op jit(solution)/shard_map/ppermute | solution.py:38
  111.2 12.9 %copy-start.13 = (bf16[8,32,2048]{2,1,0:T(8,128)(2,1)S(1)}, bf16[8,32,2048]{2,1,0:T(8,128)(2,1)}, u32[]{:S(2)}) copy-start(bf16[8,32,2048]{2,1,0:T(8,128)(2,1)} %copy-done.12) | copy-start | bytes 3145732
  111.2 12.9 %copy-start.15 = (bf16[8,32,2048]{2,1,0:T(8,128)(2,1)S(1)}, bf16[8,32,2048]{2,1,0:T(8,128)(2,1)}, u32[]{:S(2)}) copy-start(bf16[8,32,2048]{2,1,0:T(8,128)(2,1)} %copy-done.14) | copy-start | bytes 3145732
  111.2 12.9 %copy-start.17 = (bf16[8,32,2048]{2,1,0:T(8,128)(2,1)S(1)}, bf16[8,32,2048]{2,1,0:T(8,128)(2,1)}, u32[]{:S(2)}) copy-start(bf16[8,32,2048]{2,1,0:T(8,128)(2,1)} %copy-done.16) | copy-start | bytes 3145732
  111.2 12.9 %copy-start.19 = (bf16[8,32,2048]{2,1,0:T(8,128)(2,1)S(1)}, bf16[8,32,2048]{2,1,0:T(8,128)(2,1)}, u32[]{:S(2)}) copy-start(bf16[8,32,2048]{2,1,0:T(8,128)(2,1)} %copy-done.18) | copy-start | bytes 3145732
  124.0 19.3 %copy-start = (f32[1,32,16,1024]{3,2,1,0:T(8,128)S(1)}, f32[1,32,16,1024]{3,2,1,0:T(8,128)}, u32[]{:S(2)}) copy-start(f32[1,32,16,1024]{3,2,1,0:T(8,128)} %shard_map.118.f0) | copy-start | bytes 6291460
  124.0 19.3 %copy-start.5 = (bf16[8,64,1024]{2,1,0:T(8,128)(2,1)S(1)}, bf16[8,64,1024]{2,1,0:T(8,128)(2,1)}, u32[]{:S(2)}) copy-start(bf16[8,64,1024]{2,1,0:T(8,128)(2,1)} %copy-done.4) | copy-start | bytes 3145732
  149.9 5.1 %collective-permute-start.34 = (f32[8,24,128]{2,1,0:T(8,128)S(1)}, f32[8,24,128]{2,1,0:T(8,128)S(1)}, u32[]{:S(2)}, u32[]{:S(2)}) collective-permute-start(f32[8,24,128]{2,1,0:T(8,128)S(1)} %get-tuple-element.36), channel_id=1, source_target_pairs={{0,32},{2,34},{4,36},{6,38},{1,33},{3,35},{5,37},{7,39},{8,40},{10... | collective-permute-start | bytes 294920 | tf_op jit(solution)/shard_map/ppermute | solution.py:38
  150.8 7.3 %collective-permute-start.35 = (f32[8,24,128]{2,1,0:T(8,128)S(1)}, f32[8,24,128]{2,1,0:T(8,128)S(1)}, u32[]{:S(2)}, u32[]{:S(2)}) collective-permute-start(f32[8,24,128]{2,1,0:T(8,128)S(1)} %get-tuple-element.37), channel_id=1, source_target_pairs={{0,96},{2,98},{4,100},{6,102},{1,97},{3,99},{5,101},{7,103},{8,104... | collective-permute-start | bytes 294920 | tf_op jit(solution)/shard_map/ppermute | solution.py:38
  153.7 6.1 %collective-permute-start.36 = (f32[8,24,128]{2,1,0:T(8,128)S(1)}, f32[8,24,128]{2,1,0:T(8,128)S(1)}, u32[]{:S(2)}, u32[]{:S(2)}) collective-permute-start(f32[8,24,128]{2,1,0:T(8,128)S(1)} %get-tuple-element.38), channel_id=1, source_target_pairs={{0,64},{2,66},{4,68},{6,70},{1,65},{3,67},{5,69},{7,71},{8,72},{10... | collective-permute-start | bytes 294920 | tf_op jit(solution)/shard_map/ppermute | solution.py:38
  159.9 5.4 %collective-permute-start.37 = (f32[2,24,128]{2,1,0:T(8,128)S(1)}, f32[2,24,128]{2,1,0:T(8,128)S(1)}, u32[]{:S(2)}, u32[]{:S(2)}) collective-permute-start(f32[2,24,128]{2,1,0:T(8,128)S(1)} %get-tuple-element.65), channel_id=1, source_target_pairs={{0,8},{2,10},{4,12},{6,14},{1,9},{3,11},{5,13},{7,15},{8,0},{10,2}... | collective-permute-start | bytes 73736 | tf_op jit(solution)/shard_map/ppermute | solution.py:38
  160.8 5.0 %collective-permute-start.38 = (f32[2,24,128]{2,1,0:T(8,128)S(1)}, f32[2,24,128]{2,1,0:T(8,128)S(1)}, u32[]{:S(2)}, u32[]{:S(2)}) collective-permute-start(f32[2,24,128]{2,1,0:T(8,128)S(1)} %get-tuple-element.64), channel_id=1, source_target_pairs={{0,24},{2,26},{4,28},{6,30},{1,25},{3,27},{5,29},{7,31},{8,16},{10... | collective-permute-start | bytes 73736 | tf_op jit(solution)/shard_map/ppermute | solution.py:38
  164.0 5.3 %collective-permute-start.39 = (f32[2,24,128]{2,1,0:T(8,128)S(1)}, f32[2,24,128]{2,1,0:T(8,128)S(1)}, u32[]{:S(2)}, u32[]{:S(2)}) collective-permute-start(f32[2,24,128]{2,1,0:T(8,128)S(1)} %get-tuple-element.63), channel_id=1, source_target_pairs={{0,16},{2,18},{4,20},{6,22},{1,17},{3,19},{5,21},{7,23},{8,24},{10... | collective-permute-start | bytes 73736 | tf_op jit(solution)/shard_map/ppermute | solution.py:38
  169.3 5.3 %collective-permute-start.40 = (f32[24,128]{1,0:T(8,128)S(1)}, f32[24,128]{1,0:T(8,128)S(1)}, u32[]{:S(2)}, u32[]{:S(2)}) collective-permute-start(f32[24,128]{1,0:T(8,128)S(1)} %get-tuple-element.66), channel_id=1, source_target_pairs={{0,1},{2,3},{4,5},{6,7},{1,0},{3,2},{5,4},{7,6},{8,9},{10,11},{12,... | collective-permute-start | bytes 36872 | tf_op jit(solution)/shard_map/ppermute | solution.py:38
  170.5 4.1 %collective-permute-start.41 = (f32[24,128]{1,0:T(8,128)S(1)}, f32[24,128]{1,0:T(8,128)S(1)}, u32[]{:S(2)}, u32[]{:S(2)}) collective-permute-start(f32[24,128]{1,0:T(8,128)S(1)} %get-tuple-element.67), channel_id=1, source_target_pairs={{0,4},{2,6},{4,0},{6,2},{1,5},{3,7},{5,1},{7,3},{8,12},{10,14},{12... | collective-permute-start | bytes 36872 | tf_op jit(solution)/shard_map/ppermute | solution.py:38
  171.0 4.9 %collective-permute-start.42 = (f32[24,128]{1,0:T(8,128)S(1)}, f32[24,128]{1,0:T(8,128)S(1)}, u32[]{:S(2)}, u32[]{:S(2)}) collective-permute-start(f32[24,128]{1,0:T(8,128)S(1)} %get-tuple-element.67), channel_id=1, source_target_pairs={{0,5},{2,7},{4,1},{6,3},{1,4},{3,6},{5,0},{7,2},{8,13},{10,15},{12... | collective-permute-start | bytes 36872 | tf_op jit(solution)/shard_map/ppermute | solution.py:38
  (12 other events, 43.8 us)

commit v2 on v1

--- a/solution.py
+++ b/solution.py
@@ -177,7 +177,7 @@
             bands = pick(place[96 + off])
             both = lax.dot_general(left, bands, (((1,), (1,)), ((), ())), preferred_element_type=jnp.float32)
             terms = both[:48] + both[48:]
-            outs[group][unit] = jnp.concatenate([terms[:24], terms[24:]], axis=1)
+            outs[group][unit] = jnp.concatenate([terms[:24], terms[24:]], axis=1).astype(outs[group].dtype)
 
 def project(place, folded, val):
     vmem = pl.BlockSpec(memory_space=pltpu.VMEM)
@@ -186,7 +186,7 @@
         grid_spec=pltpu.PrefetchScalarGridSpec(
             num_scalar_prefetch=1, grid=(), in_specs=[vmem] * 6, out_specs=[vmem] * 4
         ),
-        out_shape=[jax.ShapeDtypeStruct((8, 24, 128), jnp.float32)] * 4,
+        out_shape=[jax.ShapeDtypeStruct((8, 24, 128), jnp.bfloat16 if k else jnp.float32) for k in range(4)],
         compiler_params=pltpu.CompilerParams(vmem_limit_bytes=14 << 20),
         cost_estimate=pl.CostEstimate(flops=800_000_000, bytes_accessed=10 << 20, transcendentals=0),
     )(place, *folded, *val)
@@ -195,7 +195,7 @@
     moves = []
     for mask in masks:
         one = tuple(mask if dim == name else 0 for name in "yzx") + (0,)
-        moves.append(send(parts[mask], [one] * 2))
+        moves.append(send(parts[mask], [one] * 2).astype(jnp.float32))
     return (parts[0] + moves[0]) + (moves[1] + moves[2])
 
 def lookup(keys, table):

time: 177 us -> 176 us (level)
  transfers between devices with their start and end apart: 43 -> 43, of which waited for: 18 -> 17; matrix products, arithmetic and copies ran while one was open for 2% -> 2% of each run, Pallas kernels for 17% -> 17%
where the time goes in v2:
time: 176 us
  waiting for transfers between devices  79.3 us (45%)
  starting transfers between devices  45 us (26%)
  Pallas kernels  35 us (20%)
  local copies, waits for them, and re-layouts  12.8 us (7%)
  other arithmetic  3.53 us (2%)
    ppermute x43, waiting for transfers between devices, send(): return lax.ppermute(value, AXES, moved(masks))  79.3 us
    ppermute x43, starting transfers between devices, send(): return lax.ppermute(value, AXES, moved(masks))  45 us
    pallas_call x2, Pallas kernels, screen(): pl.pallas_call(functools.partial(screen_kernel, parts), grid_spec=pltpu.P...  30.5 us
    unnamed x73, local copies, waits for them, and re-layouts  11.1 us
    pallas_call x1, Pallas kernels, project(): pl.pallas_call(project_kernel, grid_spec=pltpu.PrefetchScalarGridSpec(num...  4.51 us
  transfers between devices with their start and end apart: 43, of which 17 were waited for; matrix products, arithmetic and copies ran while one was open for 2% of the time, Pallas kernels for 17%

profile of v2, /device:TPU:0, one launch (start us, length us, event | category | flops | bytes accessed | tf_op | source)
XLA Modules:
  0.0 176.2 jit_solution(2573194513553020110)
XLA Ops:
  0.0 0.9 constant_dynamic-update-slice_fusion.1
  1.0 1.0 constant_dynamic-update-slice_fusion
  1.9 4.2 %collective-permute-start = (bf16[1,96,2048]{2,1,0:T(8,128)(2,1)S(1)}, bf16[1,96,2048]{2,1,0:T(8,128)(2,1)S(1)}, u32[]{:S(2)}, u32[]{:S(2)}) collective-permute-start(bf16[1,96,2048]{2,1,0:T(8,128)(2,1)S(1)} %constant_dynamic-update-slice_fusion), channel_id=1, source_target_pairs={{0,24},{2,10},{4,28},{6,14},{1,25},{3,11},{5,29},{7,15},{8,16},{10... | collective-permute-start | bytes 1179656 | tf_op jit(solution)/shard_map/ppermute | solution.py:38
  6.2 1.5 collective-permute-start.28
  7.7 3.0 %collective-permute-start.1 = (bf16[1,96,2048]{2,1,0:T(8,128)(2,1)S(1)}, bf16[1,96,2048]{2,1,0:T(8,128)(2,1)S(1)}, u32[]{:S(2)}, u32[]{:S(2)}) collective-permute-start(bf16[1,96,2048]{2,1,0:T(8,128)(2,1)S(1)} %constant_dynamic-update-slice_fusion), channel_id=1, source_target_pairs={{0,96},{2,34},{4,100},{6,38},{1,97},{3,35},{5,101},{7,39},{8,104},... | collective-permute-start | bytes 1179656 | tf_op jit(solution)/shard_map/ppermute | solution.py:38
  10.7 1.2 collective-permute-done
  11.9 3.0 %collective-permute-start.2 = (bf16[1,96,2048]{2,1,0:T(8,128)(2,1)S(1)}, bf16[1,96,2048]{2,1,0:T(8,128)(2,1)S(1)}, u32[]{:S(2)}, u32[]{:S(2)}) collective-permute-start(bf16[1,96,2048]{2,1,0:T(8,128)(2,1)S(1)} %collective-permute-done), channel_id=1, source_target_pairs={{0,96},{2,34},{4,100},{6,38},{1,97},{3,35},{5,101},{7,39},{8,104},... | collective-permute-start | bytes 1179656 | tf_op jit(solution)/shard_map/ppermute | solution.py:38
  14.9 0.9 pad_maximum_fusion.1
  15.9 3.3 %collective-permute-start.29 = (bf16[2,64,1024]{2,1,0:T(8,128)(2,1)S(1)}, bf16[2,64,1024]{2,1,0:T(8,128)(2,1)S(1)}, u32[]{:S(2)}, u32[]{:S(2)}) collective-permute-start(bf16[2,64,1024]{2,1,0:T(8,128)(2,1)S(1)} %pad_maximum_fusion.1), channel_id=1, source_target_pairs={{0,24},{2,10},{4,28},{6,14},{1,25},{3,11},{5,29},{7,15},{8,16},{10... | collective-permute-start | bytes 786440 | tf_op jit(solution)/shard_map/ppermute | solution.py:38
  19.2 4.4 %collective-permute-done.29 = bf16[2,64,1024]{2,1,0:T(8,128)(2,1)S(1)} collective-permute-done((bf16[2,64,1024]{2,1,0:T(8,128)(2,1)S(1)}, bf16[2,64,1024]{2,1,0:T(8,128)(2,1)S(1)}, u32[]{:S(2)}, u32[]{:S(2)}) %collective-permute-start.29) | collective-permute-done | bytes 262176 | tf_op jit(solution)/shard_map/ppermute | solution.py:38
  23.5 1.0 pad_maximum_fusion
  25.0 1.6 collective-permute-start.5
  26.6 0.4 collective-permute-start.4
  27.4 8.7 %collective-permute-done.30 = bf16[4,64,1024]{2,1,0:T(8,128)(2,1)S(1)} collective-permute-done((bf16[4,64,1024]{2,1,0:T(8,128)(2,1)S(1)}, bf16[4,64,1024]{2,1,0:T(8,128)(2,1)S(1)}, u32[]{:S(2)}, u32[]{:S(2)}) %collective-permute-start.30) | collective-permute-done | bytes 524320 | tf_op jit(solution)/shard_map/ppermute | solution.py:38
  36.1 1.8 %collective-permute-start.31 = (bf16[8,64,1024]{2,1,0:T(8,128)(2,1)S(1)}, bf16[8,64,1024]{2,1,0:T(8,128)(2,1)S(1)}, u32[]{:S(2)}, u32[]{:S(2)}) collective-permute-start(bf16[8,64,1024]{2,1,0:T(8,128)(2,1)S(1)} %constant_dynamic-update-slice_fusion.8.v0), channel_id=1, source_target_pairs={{0,8},{2,26},{4,12},{6,30},{1,9},{3,27},{5,13},{7,31},{8,0},{10,18... | collective-permute-start | bytes 3145736 | tf_op jit(solution)/shard_map/ppermute | solution.py:38
  38.1 0.4 collective-permute-start.14
  38.5 0.4 collective-permute-start.21
  39.1 1.9 %collective-permute-start.22 = (bf16[8,32,2048]{2,1,0:T(8,128)(2,1)S(1)}, bf16[8,32,2048]{2,1,0:T(8,128)(2,1)S(1)}, u32[]{:S(2)}, u32[]{:S(2)}) collective-permute-start(bf16[8,32,2048]{2,1,0:T(8,128)(2,1)S(1)} %constant_dynamic-update-slice_fusion.6.refs_8_), channel_id=1, source_target_pairs={{0,8},{2,26},{4,12},{6,30},{1,9},{3,27},{5,13},{7,31},{8,0},{10,18... | collective-permute-start | bytes 3145736 | tf_op jit(solution)/shard_map/ppermute | solution.py:38
  41.0 10.0 %collective-permute-done.31.v1 = bf16[8,64,1024]{2,1,0:T(8,128)(2,1)S(1)} collective-permute-done((bf16[8,64,1024]{2,1,0:T(8,128)(2,1)S(1)}, bf16[8,64,1024]{2,1,0:T(8,128)(2,1)S(1)}, u32[]{:S(2)}, u32[]{:S(2)}) %collective-permute-start.31) | collective-permute-done | bytes 1048608 | tf_op jit(solution)/shard_map/ppermute | solution.py:38
  51.0 11.2 %collective-permute-done.14.refs_1_ = bf16[8,32,2048]{2,1,0:T(8,128)(2,1)S(1)} collective-permute-done((bf16[8,32,2048]{2,1,0:T(8,128)(2,1)S(1)}, bf16[8,32,2048]{2,1,0:T(8,128)(2,1)S(1)}, u32[]{:S(2)}, u32[]{:S(2)}) %collective-permute-start.14) | collective-permute-done | bytes 1048608 | tf_op jit(solution)/shard_map/ppermute | solution.py:38
  62.3 0.5 collective-permute-start.24
  62.9 0.4 collective-permute-start.6
  63.2 10.2 %collective-permute-done.22.refs_10_ = bf16[8,32,2048]{2,1,0:T(8,128)(2,1)S(1)} collective-permute-done((bf16[8,32,2048]{2,1,0:T(8,128)(2,1)S(1)}, bf16[8,32,2048]{2,1,0:T(8,128)(2,1)S(1)}, u32[]{:S(2)}, u32[]{:S(2)}) %collective-permute-start.22) | collective-permute-done | bytes 1048608 | tf_op jit(solution)/shard_map/ppermute | solution.py:38
  73.5 0.4 collective-permute-start.7
  73.9 1.1 copy-done.12
  75.3 2.5 %collective-permute-done.6.refs_1_ = bf16[8,32,2048]{2,1,0:T(8,128)(2,1)S(1)} collective-permute-done((bf16[8,32,2048]{2,1,0:T(8,128)(2,1)S(1)}, bf16[8,32,2048]{2,1,0:T(8,128)(2,1)S(1)}, u32[]{:S(2)}, u32[]{:S(2)}) %collective-permute-start.6) | collective-permute-done | bytes 1048608 | tf_op jit(solution)/shard_map/ppermute | solution.py:38
  77.7 1.7 collective-permute-start.23
  79.5 8.9 %collective-permute-done.7.refs_2_ = bf16[8,32,2048]{2,1,0:T(8,128)(2,1)} collective-permute-done((bf16[8,32,2048]{2,1,0:T(8,128)(2,1)S(1)}, bf16[8,32,2048]{2,1,0:T(8,128)(2,1)}, u32[]{:S(2)}, u32[]{:S(2)}) %collective-permute-start.7) | collective-permute-done | bytes 1048608 | tf_op jit(solution)/shard_map/ppermute | solution.py:38
  88.4 1.0 copy-done.2
  89.4 0.5 collective-permute-start.19
  89.9 1.0 copy-done.10
  90.9 0.6 collective-permute-start.8
  91.5 1.3 collective-permute-done.23.refs_11_
  92.8 1.3 collective-permute-start.25
  94.1 1.0 copy-done.16
  95.1 1.0 copy-done.18
  96.2 0.5 collective-permute-start.11
  97.0 8.8 %collective-permute-done.8.refs_3_ = bf16[8,32,2048]{2,1,0:T(8,128)(2,1)} collective-permute-done((bf16[8,32,2048]{2,1,0:T(8,128)(2,1)S(1)}, bf16[8,32,2048]{2,1,0:T(8,128)(2,1)}, u32[]{:S(2)}, u32[]{:S(2)}) %collective-permute-start.8) | collective-permute-done | bytes 1048608 | tf_op jit(solution)/shard_map/ppermute | solution.py:38
  106.3 0.5 collective-permute-start.26
  107.0 0.4 collective-permute-start.27
  108.2 0.6 collective-permute-done.12.refs_7_
  108.8 1.2 collective-permute-start.32
  110.0 1.2 copy-done.3
  111.2 12.8 %shard_map.118.f0 = f32[1,32,16,1024]{3,2,1,0:T(8,128)} custom-call(s32[193]{0:T(256)S(1)} %pad_add_fusion.rows, bf16[8,32,2048]{2,1,0:T(8,128)(2,1)S(1)} %constant_dynamic-update-slice_fusion.2.refs_0_, bf16[8,32,2048]{2,1,0:T(8,128)(2,1)S(1)} %collective-permute-done.6.refs_1_, bf16[8,32,2048]{2,1,0:T(8,128)(2,1)} %collective-permute-done.7.refs_2_, ...), custom_call_target="tpu_custom_call" | custom-call | flops 4300000256 | bytes 8388608 | tf_op jit(solution)/shard_map/pallas_call | solution.py:138
  124.1 1.4 copy-done.11
  125.5 17.8 %shard_map.119.f21 = f32[2,32,16,1024]{3,2,1,0:T(8,128)} custom-call(s32[193]{0:T(256)S(1)} %pad_add_fusion.rows, bf16[8,32,2048]{2,1,0:T(8,128)(2,1)S(1)} %copy-done.7, bf16[8,32,2048]{2,1,0:T(8,128)(2,1)S(1)} %copy-done.9, bf16[8,32,2048]{2,1,0:T(8,128)(2,1)S(1)} %copy-done.11, bf16[8,32,2048]{2,1,0:T(8,128)(2,1)S(1)} %copy-done.15, ...), custom_call_target="tpu_custom_call" | custom-call | flops 8600000512 | bytes 8388608 | tf_op jit(solution)/shard_map/pallas_call | solution.py:138
  143.3 2.2 %copy-done.1 = f32[2,32,16,1024]{3,2,1,0:T(8,128)S(1)} copy-done((f32[2,32,16,1024]{3,2,1,0:T(8,128)S(1)}, f32[2,32,16,1024]{3,2,1,0:T(8,128)}, u32[]{:S(2)}) %copy-start.1) | copy-done | bytes 4194328
  145.5 4.5 %shard_map.120 = (f32[8,24,128]{2,1,0:T(8,128)S(1)}, bf16[8,24,128]{2,1,0:T(8,128)(2,1)S(1)}, bf16[8,24,128]{2,1,0:T(8,128)(2,1)S(1)}, bf16[8,24,128]{2,1,0:T(8,128)(2,1)S(1)}) custom-call(s32[128]{0:T(128)S(1)} %reshape.27.place, f32[1,32,16,1024]{3,2,1,0:T(8,128)S(1)} %copy-done, f32[2,32,16,1024]{3,2,1,0:T(8,128)S(1)} %copy-done.1, ...), custom_call_target="tpu_custom_call" | custom-call | flops 800000000 | bytes 10485760 | tf_op jit(solution)/shard_map/pallas_call | solution.py:184
  150.0 0.9 collective-permute-start.34
  150.9 3.0 %collective-permute-start.35 = (bf16[8,24,128]{2,1,0:T(8,128)(2,1)S(1)}, bf16[8,24,128]{2,1,0:T(8,128)(2,1)S(1)}, u32[]{:S(2)}, u32[]{:S(2)}) collective-permute-start(bf16[8,24,128]{2,1,0:T(8,128)(2,1)S(1)} %get-tuple-element.37), channel_id=1, source_target_pairs={{0,96},{2,98},{4,100},{6,102},{1,97},{3,99},{5,101},{7,103},{8,104... | collective-permute-start | bytes 147464 | tf_op jit(solution)/shard_map/ppermute | solution.py:38
  153.9 0.6 collective-permute-start.36
  154.4 2.2 %collective-permute-done.35 = bf16[8,24,128]{2,1,0:T(8,128)(2,1)S(1)} collective-permute-done((bf16[8,24,128]{2,1,0:T(8,128)(2,1)S(1)}, bf16[8,24,128]{2,1,0:T(8,128)(2,1)S(1)}, u32[]{:S(2)}, u32[]{:S(2)}) %collective-permute-start.35) | collective-permute-done | bytes 49184 | tf_op jit(solution)/shard_map/ppermute | solution.py:38
  156.6 2.8 %collective-permute-done.36 = bf16[8,24,128]{2,1,0:T(8,128)(2,1)S(1)} collective-permute-done((bf16[8,24,128]{2,1,0:T(8,128)(2,1)S(1)}, bf16[8,24,128]{2,1,0:T(8,128)(2,1)S(1)}, u32[]{:S(2)}, u32[]{:S(2)}) %collective-permute-start.36) | collective-permute-done | bytes 49184 | tf_op jit(solution)/shard_map/ppermute | solution.py:38
  159.5 0.7 collective-permute-start.37
  160.2 3.3 %collective-permute-start.38 = (f32[2,24,128]{2,1,0:T(8,128)S(1)}, f32[2,24,128]{2,1,0:T(8,128)S(1)}, u32[]{:S(2)}, u32[]{:S(2)}) collective-permute-start(f32[2,24,128]{2,1,0:T(8,128)S(1)} %get-tuple-element.64), channel_id=1, source_target_pairs={{0,24},{2,26},{4,28},{6,30},{1,25},{3,27},{5,29},{7,31},{8,16},{10... | collective-permute-start | bytes 73736 | tf_op jit(solution)/shard_map/ppermute | solution.py:38
  163.5 1.4 collective-permute-start.39
  164.9 0.4 collective-permute-done.38
  165.3 3.5 %collective-permute-done.39 = f32[2,24,128]{2,1,0:T(8,128)S(1)} collective-permute-done((f32[2,24,128]{2,1,0:T(8,128)S(1)}, f32[2,24,128]{2,1,0:T(8,128)S(1)}, u32[]{:S(2)}, u32[]{:S(2)}) %collective-permute-start.39) | collective-permute-done | bytes 24608 | tf_op jit(solution)/shard_map/ppermute | solution.py:38
  168.9 1.2 collective-permute-start.40
  170.1 0.6 collective-permute-start.41
  170.6 2.4 %collective-permute-start.42 = (f32[24,128]{1,0:T(8,128)S(1)}, f32[24,128]{1,0:T(8,128)S(1)}, u32[]{:S(2)}, u32[]{:S(2)}) collective-permute-start(f32[24,128]{1,0:T(8,128)S(1)} %get-tuple-element.67), channel_id=1, source_target_pairs={{0,5},{2,7},{4,1},{6,3},{1,4},{3,6},{5,0},{7,2},{8,13},{10,15},{12... | collective-permute-start | bytes 36872 | tf_op jit(solution)/shard_map/ppermute | solution.py:38
  173.0 1.1 collective-permute-done.40
  174.2 1.4 collective-permute-done.42
  175.6 0.6 maximum_bitcast_fusion
  (130 shorter events, 3.6 us)
Async XLA Ops:
  0.9 26.3 %copy-start.20 = (bf16[1,64,1024]{2,1,0:T(8,128)(2,1)S(1)}, bf16[1,64,1024]{2,1,0:T(8,128)(2,1)}, u32[]{:S(2)}) copy-start(bf16[1,64,1024]{2,1,0:T(8,128)(2,1)} %param.14) | copy-start | bytes 393220
  1.9 10.0 %collective-permute-start = (bf16[1,96,2048]{2,1,0:T(8,128)(2,1)S(1)}, bf16[1,96,2048]{2,1,0:T(8,128)(2,1)S(1)}, u32[]{:S(2)}, u32[]{:S(2)}) collective-permute-start(bf16[1,96,2048]{2,1,0:T(8,128)(2,1)S(1)} %constant_dynamic-update-slice_fusion), channel_id=1, source_target_pairs={{0,24},{2,10},{4,28},{6,14},{1,25},{3,11},{5,29},{7,15},{8,16},{10... | collective-permute-start | bytes 1179656 | tf_op jit(solution)/shard_map/ppermute | solution.py:38
  6.2 8.8 %collective-permute-start.28 = (bf16[1,64,1024]{2,1,0:T(8,128)(2,1)}, bf16[1,64,1024]{2,1,0:T(8,128)(2,1)S(1)}, u32[]{:S(2)}, u32[]{:S(2)}) collective-permute-start(bf16[1,64,1024]{2,1,0:T(8,128)(2,1)} %param.14), channel_id=1, source_target_pairs={{0,4},{2,6},{4,0},{6,2},{1,5},{3,7},{5,1},{7,3},{8,12},{10,14},{12... | collective-permute-start | bytes 393224 | tf_op jit(solution)/shard_map/ppermute | solution.py:38
  7.7 17.1 %collective-permute-start.1 = (bf16[1,96,2048]{2,1,0:T(8,128)(2,1)S(1)}, bf16[1,96,2048]{2,1,0:T(8,128)(2,1)S(1)}, u32[]{:S(2)}, u32[]{:S(2)}) collective-permute-start(bf16[1,96,2048]{2,1,0:T(8,128)(2,1)S(1)} %constant_dynamic-update-slice_fusion), channel_id=1, source_target_pairs={{0,96},{2,34},{4,100},{6,38},{1,97},{3,35},{5,101},{7,39},{8,104},... | collective-permute-start | bytes 1179656 | tf_op jit(solution)/shard_map/ppermute | solution.py:38
  11.9 12.9 %collective-permute-start.2 = (bf16[1,96,2048]{2,1,0:T(8,128)(2,1)S(1)}, bf16[1,96,2048]{2,1,0:T(8,128)(2,1)S(1)}, u32[]{:S(2)}, u32[]{:S(2)}) collective-permute-start(bf16[1,96,2048]{2,1,0:T(8,128)(2,1)S(1)} %collective-permute-done), channel_id=1, source_target_pairs={{0,96},{2,34},{4,100},{6,38},{1,97},{3,35},{5,101},{7,39},{8,104},... | collective-permute-start | bytes 1179656 | tf_op jit(solution)/shard_map/ppermute | solution.py:38
  15.9 7.7 %collective-permute-start.29 = (bf16[2,64,1024]{2,1,0:T(8,128)(2,1)S(1)}, bf16[2,64,1024]{2,1,0:T(8,128)(2,1)S(1)}, u32[]{:S(2)}, u32[]{:S(2)}) collective-permute-start(bf16[2,64,1024]{2,1,0:T(8,128)(2,1)S(1)} %pad_maximum_fusion.1), channel_id=1, source_target_pairs={{0,24},{2,10},{4,28},{6,14},{1,25},{3,11},{5,29},{7,15},{8,16},{10... | collective-permute-start | bytes 786440 | tf_op jit(solution)/shard_map/ppermute | solution.py:38
  24.5 11.6 %collective-permute-start.30 = (bf16[4,64,1024]{2,1,0:T(8,128)(2,1)S(1)}, bf16[4,64,1024]{2,1,0:T(8,128)(2,1)S(1)}, u32[]{:S(2)}, u32[]{:S(2)}) collective-permute-start(bf16[4,64,1024]{2,1,0:T(8,128)(2,1)S(1)} %pad_maximum_fusion), channel_id=1, source_target_pairs={{0,96},{2,34},{4,100},{6,38},{1,97},{3,35},{5,101},{7,39},{8,104},... | collective-permute-start | bytes 1572872 | tf_op jit(solution)/shard_map/ppermute | solution.py:38
  25.0 12.9 %collective-permute-start.5 = (bf16[4,32,2048]{2,1,0:T(8,128)(2,1)S(1)}, bf16[4,32,2048]{2,1,0:T(8,128)(2,1)S(1)}, u32[]{:S(2)}, u32[]{:S(2)}) collective-permute-start(bf16[4,32,2048]{2,1,0:T(8,128)(2,1)S(1)} %maximum_maximum_fusion.2), channel_id=1, source_target_pairs={{0,4},{2,7},{4,0},{6,3},{1,5},{3,6},{5,1},{7,2},{8,12},{10,15},{12... | collective-permute-start | bytes 1572872 | tf_op jit(solution)/shard_map/ppermute | solution.py:38
  26.6 11.3 %collective-permute-start.4 = (bf16[4,32,2048]{2,1,0:T(8,128)(2,1)S(1)}, bf16[4,32,2048]{2,1,0:T(8,128)(2,1)S(1)}, u32[]{:S(2)}, u32[]{:S(2)}) collective-permute-start(bf16[4,32,2048]{2,1,0:T(8,128)(2,1)S(1)} %maximum_maximum_fusion.1), channel_id=1, source_target_pairs={{0,32},{2,98},{4,36},{6,102},{1,33},{3,99},{5,37},{7,103},{8,40},{... | collective-permute-start | bytes 1572872 | tf_op jit(solution)/shard_map/ppermute | solution.py:38
  27.1 69.6 %copy-start.29 = (s32[64]{0:T(128)S(1)}, s32[64]{0:T(128)}, u32[]{:S(2)}) copy-start(s32[64]{0:T(128)} %param.17) | copy-start | bytes 772
  27.1 69.8 %copy-start.27 = (s32[3,32]{1,0:T(4,128)S(1)}, s32[3,32]{1,0:T(4,128)}, u32[]{:S(2)}) copy-start(s32[3,32]{1,0:T(4,128)} %constant.53.clone) | copy-start | bytes 1156
  27.1 69.8 %copy-start.28 = (s32[3,32]{1,0:T(4,128)S(1)}, s32[3,32]{1,0:T(4,128)}, u32[]{:S(2)}) copy-start(s32[3,32]{1,0:T(4,128)} %constant.54.clone) | copy-start | bytes 1156
  27.1 78.7 %copy-start.22 = (s32[64,64]{1,0:T(8,128)S(1)}, s32[64,64]{1,0:T(8,128)}, u32[]{:S(2)}) copy-start(s32[64,64]{1,0:T(8,128)} %param.16) | copy-start | bytes 49156
  27.2 80.2 %copy-start.25 = (s32[3,64]{1,0:T(4,128)S(1)}, s32[3,64]{1,0:T(4,128)}, u32[]{:S(2)}) copy-start(s32[3,64]{1,0:T(4,128)} %constant.55.clone) | copy-start | bytes 2308
  27.2 80.2 %copy-start.26 = (s32[3,64]{1,0:T(4,128)S(1)}, s32[3,64]{1,0:T(4,128)}, u32[]{:S(2)}) copy-start(s32[3,64]{1,0:T(4,128)} %constant.56.clone) | copy-start | bytes 2308
  27.2 10.8 %collective-permute-start.3 = (bf16[4,32,2048]{2,1,0:T(8,128)(2,1)S(1)}, bf16[4,32,2048]{2,1,0:T(8,128)(2,1)S(1)}, u32[]{:S(2)}, u32[]{:S(2)}) collective-permute-start(bf16[4,32,2048]{2,1,0:T(8,128)(2,1)S(1)} %maximum_maximum_fusion), channel_id=1, source_target_pairs={{0,8},{2,26},{4,12},{6,30},{1,9},{3,27},{5,13},{7,31},{8,0},{10,18... | collective-permute-start | bytes 1572872 | tf_op jit(solution)/shard_map/ppermute | solution.py:38
  27.3 80.4 %copy-start.23 = (s32[4,32]{1,0:T(4,128)S(1)}, s32[4,32]{1,0:T(4,128)}, u32[]{:S(2)}) copy-start(s32[4,32]{1,0:T(4,128)} %constant.57.clone) | copy-start | bytes 1540
  27.3 80.4 %copy-start.24 = (s32[4,32]{1,0:T(4,128)S(1)}, s32[4,32]{1,0:T(4,128)}, u32[]{:S(2)}) copy-start(s32[4,32]{1,0:T(4,128)} %constant.58.clone) | copy-start | bytes 1540
  36.1 14.9 %collective-permute-start.31 = (bf16[8,64,1024]{2,1,0:T(8,128)(2,1)S(1)}, bf16[8,64,1024]{2,1,0:T(8,128)(2,1)S(1)}, u32[]{:S(2)}, u32[]{:S(2)}) collective-permute-start(bf16[8,64,1024]{2,1,0:T(8,128)(2,1)S(1)} %constant_dynamic-update-slice_fusion.8.v0), channel_id=1, source_target_pairs={{0,8},{2,26},{4,12},{6,30},{1,9},{3,27},{5,13},{7,31},{8,0},{10,18... | collective-permute-start | bytes 3145736 | tf_op jit(solution)/shard_map/ppermute | solution.py:38
  38.1 56.0 %copy-start.6 = (bf16[8,32,2048]{2,1,0:T(8,128)(2,1)}, bf16[8,32,2048]{2,1,0:T(8,128)(2,1)S(1)}, u32[]{:S(2)}) copy-start(bf16[8,32,2048]{2,1,0:T(8,128)(2,1)S(1)} %constant_dynamic-update-slice_fusion.4.refs_0_) | copy-start | bytes 3145732
  38.1 24.2 %collective-permute-start.14 = (bf16[8,32,2048]{2,1,0:T(8,128)(2,1)S(1)}, bf16[8,32,2048]{2,1,0:T(8,128)(2,1)S(1)}, u32[]{:S(2)}, u32[]{:S(2)}) collective-permute-start(bf16[8,32,2048]{2,1,0:T(8,128)(2,1)S(1)} %constant_dynamic-update-slice_fusion.4.refs_0_), channel_id=1, source_target_pairs={{0,8},{2,26},{4,12},{6,30},{1,9},{3,27},{5,13},{7,31},{8,0},{10,18... | collective-permute-start | bytes 3145736 | tf_op jit(solution)/shard_map/ppermute | solution.py:38
  38.5 58.1 %copy-start.21 = (bf16[8,32,2048]{2,1,0:T(8,128)(2,1)}, bf16[8,32,2048]{2,1,0:T(8,128)(2,1)S(1)}, u32[]{:S(2)}) copy-start(bf16[8,32,2048]{2,1,0:T(8,128)(2,1)S(1)} %constant_dynamic-update-slice_fusion.6.refs_8_) | copy-start | bytes 3145732
  38.5 23.7 %collective-permute-start.21 = (bf16[8,32,2048]{2,1,0:T(8,128)(2,1)S(1)}, bf16[8,32,2048]{2,1,0:T(8,128)(2,1)}, u32[]{:S(2)}, u32[]{:S(2)}) collective-permute-start(bf16[8,32,2048]{2,1,0:T(8,128)(2,1)S(1)} %constant_dynamic-update-slice_fusion.6.refs_8_), channel_id=1, source_target_pairs={{0,4},{2,7},{4,0},{6,3},{1,5},{3,6},{5,1},{7,2},{8,12},{10,15},{12... | collective-permute-start | bytes 3145736 | tf_op jit(solution)/shard_map/ppermute | solution.py:38
  39.0 23.9 %collective-permute-start.15 = (bf16[8,32,2048]{2,1,0:T(8,128)(2,1)S(1)}, bf16[8,32,2048]{2,1,0:T(8,128)(2,1)S(1)}, u32[]{:S(2)}, u32[]{:S(2)}) collective-permute-start(bf16[8,32,2048]{2,1,0:T(8,128)(2,1)S(1)} %constant_dynamic-update-slice_fusion.4.refs_0_), channel_id=1, source_target_pairs={{0,32},{2,98},{4,36},{6,102},{1,33},{3,99},{5,37},{7,103},{8,40},{... | collective-permute-start | bytes 3145736 | tf_op jit(solution)/shard_map/ppermute | solution.py:38
  39.1 34.3 %collective-permute-start.22 = (bf16[8,32,2048]{2,1,0:T(8,128)(2,1)S(1)}, bf16[8,32,2048]{2,1,0:T(8,128)(2,1)S(1)}, u32[]{:S(2)}, u32[]{:S(2)}) collective-permute-start(bf16[8,32,2048]{2,1,0:T(8,128)(2,1)S(1)} %constant_dynamic-update-slice_fusion.6.refs_8_), channel_id=1, source_target_pairs={{0,8},{2,26},{4,12},{6,30},{1,9},{3,27},{5,13},{7,31},{8,0},{10,18... | collective-permute-start | bytes 3145736 | tf_op jit(solution)/shard_map/ppermute | solution.py:38
  51.0 43.0 %copy-start.4 = (bf16[8,64,1024]{2,1,0:T(8,128)(2,1)}, bf16[8,64,1024]{2,1,0:T(8,128)(2,1)S(1)}, u32[]{:S(2)}) copy-start(bf16[8,64,1024]{2,1,0:T(8,128)(2,1)S(1)} %collective-permute-done.31.v1) | copy-start | bytes 3145732
  51.0 22.8 %collective-permute-start.17 = (bf16[8,32,2048]{2,1,0:T(8,128)(2,1)S(1)}, bf16[8,32,2048]{2,1,0:T(8,128)(2,1)S(1)}, u32[]{:S(2)}, u32[]{:S(2)}) collective-permute-start(bf16[8,32,2048]{2,1,0:T(8,128)(2,1)S(1)} %constant_dynamic-update-slice_fusion.4.refs_0_), channel_id=1, source_target_pairs={{0,2},{2,0},{4,6},{6,4},{1,3},{3,1},{5,7},{7,5},{8,10},{10,8},{12,... | collective-permute-start | bytes 3145736 | tf_op jit(solution)/shard_map/ppermute | solution.py:38
  62.2 32.9 %copy-start.8 = (bf16[8,32,2048]{2,1,0:T(8,128)(2,1)}, bf16[8,32,2048]{2,1,0:T(8,128)(2,1)S(1)}, u32[]{:S(2)}) copy-start(bf16[8,32,2048]{2,1,0:T(8,128)(2,1)S(1)} %collective-permute-done.14.refs_1_) | copy-start | bytes 3145732
  62.3 45.7 %collective-permute-start.13 = (bf16[2048,1024]{1,0:T(8,128)(2,1)}, bf16[2048,1024]{1,0:T(8,128)(2,1)}, u32[]{:S(2)}, u32[]{:S(2)}) collective-permute-start(bf16[2048,1024]{1,0:T(8,128)(2,1)} %bitcast.1.refs_8_.refs_16_), channel_id=1, source_target_pairs={{0,2},{2,0},{4,6},{6,4},{1,3},{3,1},{5,7},{7,5},{8,10},{10,8},{12,... | collective-permute-start | bytes 12582920 | tf_op jit(solution)/shard_map/ppermute | solution.py:38
  62.3 12.7 %collective-permute-start.24 = (bf16[8,32,2048]{2,1,0:T(8,128)(2,1)S(1)}, bf16[8,32,2048]{2,1,0:T(8,128)(2,1)S(1)}, u32[]{:S(2)}, u32[]{:S(2)}) collective-permute-start(bf16[8,32,2048]{2,1,0:T(8,128)(2,1)S(1)} %constant_dynamic-update-slice_fusion.6.refs_8_), channel_id=1, source_target_pairs={{0,2},{2,0},{4,6},{6,4},{1,3},{3,1},{5,7},{7,5},{8,10},{10,8},{12,... | collective-permute-start | bytes 3145736 | tf_op jit(solution)/shard_map/ppermute | solution.py:38
  62.9 14.9 %collective-permute-start.6 = (bf16[8,32,2048]{2,1,0:T(8,128)(2,1)S(1)}, bf16[8,32,2048]{2,1,0:T(8,128)(2,1)S(1)}, u32[]{:S(2)}, u32[]{:S(2)}) collective-permute-start(bf16[8,32,2048]{2,1,0:T(8,128)(2,1)S(1)} %constant_dynamic-update-slice_fusion.2.refs_0_), channel_id=1, source_target_pairs={{0,32},{2,98},{4,36},{6,102},{1,33},{3,99},{5,37},{7,103},{8,40},{... | collective-permute-start | bytes 3145736 | tf_op jit(solution)/shard_map/ppermute | solution.py:38
  73.5 23.2 %copy-start.30 = (bf16[8,32,2048]{2,1,0:T(8,128)(2,1)}, bf16[8,32,2048]{2,1,0:T(8,128)(2,1)S(1)}, u32[]{:S(2)}) copy-start(bf16[8,32,2048]{2,1,0:T(8,128)(2,1)S(1)} %collective-permute-done.22.refs_10_) | copy-start | bytes 3145732
  73.5 14.9 %collective-permute-start.7 = (bf16[8,32,2048]{2,1,0:T(8,128)(2,1)S(1)}, bf16[8,32,2048]{2,1,0:T(8,128)(2,1)}, u32[]{:S(2)}, u32[]{:S(2)}) collective-permute-start(bf16[8,32,2048]{2,1,0:T(8,128)(2,1)S(1)} %constant_dynamic-update-slice_fusion.2.refs_0_), channel_id=1, source_target_pairs={{0,4},{2,7},{4,0},{6,3},{1,5},{3,6},{5,1},{7,2},{8,12},{10,15},{12... | collective-permute-start | bytes 3145736 | tf_op jit(solution)/shard_map/ppermute | solution.py:38
  74.9 13.5 %collective-permute-start.9 = (bf16[8,32,2048]{2,1,0:T(8,128)(2,1)S(1)}, bf16[8,32,2048]{2,1,0:T(8,128)(2,1)S(1)}, u32[]{:S(2)}, u32[]{:S(2)}) collective-permute-start(bf16[8,32,2048]{2,1,0:T(8,128)(2,1)S(1)} %constant_dynamic-update-slice_fusion.2.refs_0_), channel_id=1, source_target_pairs={{0,2},{2,0},{4,6},{6,4},{1,3},{3,1},{5,7},{7,5},{8,10},{10,8},{12,... | collective-permute-start | bytes 3145736 | tf_op jit(solution)/shard_map/ppermute | solution.py:38
  74.9 21.7 %copy-start.31 = (bf16[8,32,2048]{2,1,0:T(8,128)(2,1)}, bf16[8,32,2048]{2,1,0:T(8,128)(2,1)S(1)}, u32[]{:S(2)}) copy-start(bf16[8,32,2048]{2,1,0:T(8,128)(2,1)S(1)} %collective-permute-done.24.refs_12_) | copy-start | bytes 3145732
  74.9 16.0 %collective-permute-start.16 = (bf16[8,32,2048]{2,1,0:T(8,128)(2,1)S(1)}, bf16[8,32,2048]{2,1,0:T(8,128)(2,1)S(1)}, u32[]{:S(2)}, u32[]{:S(2)}) collective-permute-start(bf16[8,32,2048]{2,1,0:T(8,128)(2,1)S(1)} %collective-permute-done.14.refs_1_), channel_id=1, source_target_pairs={{0,32},{2,98},{4,36},{6,102},{1,33},{3,99},{5,37},{7,103},{8,40},{... | collective-permute-start | bytes 3145736 | tf_op jit(solution)/shard_map/ppermute | solution.py:38
  77.7 15.0 %collective-permute-start.23 = (bf16[8,32,2048]{2,1,0:T(8,128)(2,1)}, bf16[8,32,2048]{2,1,0:T(8,128)(2,1)S(1)}, u32[]{:S(2)}, u32[]{:S(2)}) collective-permute-start(bf16[8,32,2048]{2,1,0:T(8,128)(2,1)} %collective-permute-done.21.refs_9_), channel_id=1, source_target_pairs={{0,8},{2,26},{4,12},{6,30},{1,9},{3,27},{5,13},{7,31},{8,0},{10,18... | collective-permute-start | bytes 3145736 | tf_op jit(solution)/shard_map/ppermute | solution.py:38
  88.4 5.7 %collective-permute-start.18 = (bf16[8,32,2048]{2,1,0:T(8,128)(2,1)S(1)}, bf16[8,32,2048]{2,1,0:T(8,128)(2,1)S(1)}, u32[]{:S(2)}, u32[]{:S(2)}) collective-permute-start(bf16[8,32,2048]{2,1,0:T(8,128)(2,1)S(1)} %collective-permute-done.14.refs_1_), channel_id=1, source_target_pairs={{0,2},{2,0},{4,6},{6,4},{1,3},{3,1},{5,7},{7,5},{8,10},{10,8},{12,... | collective-permute-start | bytes 3145736 | tf_op jit(solution)/shard_map/ppermute | solution.py:38
  89.4 5.8 %collective-permute-start.19 = (bf16[8,32,2048]{2,1,0:T(8,128)(2,1)S(1)}, bf16[8,32,2048]{2,1,0:T(8,128)(2,1)S(1)}, u32[]{:S(2)}, u32[]{:S(2)}) collective-permute-start(bf16[8,32,2048]{2,1,0:T(8,128)(2,1)S(1)} %collective-permute-done.15.refs_2_), channel_id=1, source_target_pairs={{0,2},{2,0},{4,6},{6,4},{1,3},{3,1},{5,7},{7,5},{8,10},{10,8},{12,... | collective-permute-start | bytes 3145736 | tf_op jit(solution)/shard_map/ppermute | solution.py:38
  90.9 14.9 %collective-permute-start.8 = (bf16[8,32,2048]{2,1,0:T(8,128)(2,1)S(1)}, bf16[8,32,2048]{2,1,0:T(8,128)(2,1)}, u32[]{:S(2)}, u32[]{:S(2)}) collective-permute-start(bf16[8,32,2048]{2,1,0:T(8,128)(2,1)S(1)} %collective-permute-done.6.refs_1_), channel_id=1, source_target_pairs={{0,4},{2,7},{4,0},{6,3},{1,5},{3,6},{5,1},{7,2},{8,12},{10,15},{12... | collective-permute-start | bytes 3145736 | tf_op jit(solution)/shard_map/ppermute | solution.py:38
  92.8 13.6 %collective-permute-start.25 = (bf16[8,32,2048]{2,1,0:T(8,128)(2,1)}, bf16[8,32,2048]{2,1,0:T(8,128)(2,1)}, u32[]{:S(2)}, u32[]{:S(2)}) collective-permute-start(bf16[8,32,2048]{2,1,0:T(8,128)(2,1)} %collective-permute-done.21.refs_9_), channel_id=1, source_target_pairs={{0,2},{2,0},{4,6},{6,4},{1,3},{3,1},{5,7},{7,5},{8,10},{10,8},{12,... | collective-permute-start | bytes 3145736 | tf_op jit(solution)/shard_map/ppermute | solution.py:38
  95.1 11.8 %collective-permute-start.10 = (bf16[8,32,2048]{2,1,0:T(8,128)(2,1)S(1)}, bf16[8,32,2048]{2,1,0:T(8,128)(2,1)}, u32[]{:S(2)}, u32[]{:S(2)}) collective-permute-start(bf16[8,32,2048]{2,1,0:T(8,128)(2,1)S(1)} %collective-permute-done.6.refs_1_), channel_id=1, source_target_pairs={{0,2},{2,0},{4,6},{6,4},{1,3},{3,1},{5,7},{7,5},{8,10},{10,8},{12,... | collective-permute-start | bytes 3145736 | tf_op jit(solution)/shard_map/ppermute | solution.py:38
  96.2 10.8 %collective-permute-start.11 = (bf16[8,32,2048]{2,1,0:T(8,128)(2,1)}, bf16[8,32,2048]{2,1,0:T(8,128)(2,1)}, u32[]{:S(2)}, u32[]{:S(2)}) collective-permute-start(bf16[8,32,2048]{2,1,0:T(8,128)(2,1)} %collective-permute-done.7.refs_2_), channel_id=1, source_target_pairs={{0,2},{2,0},{4,6},{6,4},{1,3},{3,1},{5,7},{7,5},{8,10},{10,8},{12,... | collective-permute-start | bytes 3145736 | tf_op jit(solution)/shard_map/ppermute | solution.py:38
  105.8 3.0 %collective-permute-start.12 = (bf16[8,32,2048]{2,1,0:T(8,128)(2,1)}, bf16[8,32,2048]{2,1,0:T(8,128)(2,1)}, u32[]{:S(2)}, u32[]{:S(2)}) collective-permute-start(bf16[8,32,2048]{2,1,0:T(8,128)(2,1)} %collective-permute-done.8.refs_3_), channel_id=1, source_target_pairs={{0,2},{2,0},{4,6},{6,4},{1,3},{3,1},{5,7},{7,5},{8,10},{10,8},{12,... | collective-permute-start | bytes 3145736 | tf_op jit(solution)/shard_map/ppermute | solution.py:38
  106.3 17.7 %collective-permute-start.26 = (bf16[8,32,2048]{2,1,0:T(8,128)(2,1)}, bf16[8,32,2048]{2,1,0:T(8,128)(2,1)}, u32[]{:S(2)}, u32[]{:S(2)}) collective-permute-start(bf16[8,32,2048]{2,1,0:T(8,128)(2,1)} %copy-done.30), channel_id=1, source_target_pairs={{0,2},{2,0},{4,6},{6,4},{1,3},{3,1},{5,7},{7,5},{8,10},{10,8},{12,... | collective-permute-start | bytes 3145736 | tf_op jit(solution)/shard_map/ppermute | solution.py:38
  106.8 17.2 %collective-permute-start.20 = (bf16[8,32,2048]{2,1,0:T(8,128)(2,1)}, bf16[8,32,2048]{2,1,0:T(8,128)(2,1)}, u32[]{:S(2)}, u32[]{:S(2)}) collective-permute-start(bf16[8,32,2048]{2,1,0:T(8,128)(2,1)} %copy-done.14), channel_id=1, source_target_pairs={{0,2},{2,0},{4,6},{6,4},{1,3},{3,1},{5,7},{7,5},{8,10},{10,8},{12,... | collective-permute-start | bytes 3145736 | tf_op jit(solution)/shard_map/ppermute | solution.py:38
  107.0 17.1 %collective-permute-start.27 = (bf16[8,32,2048]{2,1,0:T(8,128)(2,1)}, bf16[8,32,2048]{2,1,0:T(8,128)(2,1)}, u32[]{:S(2)}, u32[]{:S(2)}) collective-permute-start(bf16[8,32,2048]{2,1,0:T(8,128)(2,1)} %copy-done.32), channel_id=1, source_target_pairs={{0,2},{2,0},{4,6},{6,4},{1,3},{3,1},{5,7},{7,5},{8,10},{10,8},{12,... | collective-permute-start | bytes 3145736 | tf_op jit(solution)/shard_map/ppermute | solution.py:38
  107.9 35.3 %collective-permute-start.33 = (bf16[8,64,1024]{2,1,0:T(8,128)(2,1)S(1)}, bf16[8,64,1024]{2,1,0:T(8,128)(2,1)S(1)}, u32[]{:S(2)}, u32[]{:S(2)}) collective-permute-start(bf16[8,64,1024]{2,1,0:T(8,128)(2,1)S(1)} %constant_dynamic-update-slice_fusion.8.v0), channel_id=1, source_target_pairs={{0,32},{2,98},{4,36},{6,102},{1,33},{3,99},{5,37},{7,103},{8,40},{... | collective-permute-start | bytes 3145736 | tf_op jit(solution)/shard_map/ppermute | solution.py:38
  108.8 34.5 %collective-permute-start.32 = (bf16[8,64,1024]{2,1,0:T(8,128)(2,1)}, bf16[8,64,1024]{2,1,0:T(8,128)(2,1)S(1)}, u32[]{:S(2)}, u32[]{:S(2)}) collective-permute-start(bf16[8,64,1024]{2,1,0:T(8,128)(2,1)} %copy-done.4), channel_id=1, source_target_pairs={{0,32},{2,98},{4,36},{6,102},{1,33},{3,99},{5,37},{7,103},{8,40},{... | collective-permute-start | bytes 3145736 | tf_op jit(solution)/shard_map/ppermute | solution.py:38
  111.2 12.9 %copy-start.13 = (bf16[8,32,2048]{2,1,0:T(8,128)(2,1)S(1)}, bf16[8,32,2048]{2,1,0:T(8,128)(2,1)}, u32[]{:S(2)}) copy-start(bf16[8,32,2048]{2,1,0:T(8,128)(2,1)} %copy-done.12) | copy-start | bytes 3145732
  111.2 12.9 %copy-start.15 = (bf16[8,32,2048]{2,1,0:T(8,128)(2,1)S(1)}, bf16[8,32,2048]{2,1,0:T(8,128)(2,1)}, u32[]{:S(2)}) copy-start(bf16[8,32,2048]{2,1,0:T(8,128)(2,1)} %copy-done.14) | copy-start | bytes 3145732
  111.2 12.9 %copy-start.17 = (bf16[8,32,2048]{2,1,0:T(8,128)(2,1)S(1)}, bf16[8,32,2048]{2,1,0:T(8,128)(2,1)}, u32[]{:S(2)}) copy-start(bf16[8,32,2048]{2,1,0:T(8,128)(2,1)} %copy-done.16) | copy-start | bytes 3145732
  111.2 12.9 %copy-start.19 = (bf16[8,32,2048]{2,1,0:T(8,128)(2,1)S(1)}, bf16[8,32,2048]{2,1,0:T(8,128)(2,1)}, u32[]{:S(2)}) copy-start(bf16[8,32,2048]{2,1,0:T(8,128)(2,1)} %copy-done.18) | copy-start | bytes 3145732
  124.0 19.3 %copy-start = (f32[1,32,16,1024]{3,2,1,0:T(8,128)S(1)}, f32[1,32,16,1024]{3,2,1,0:T(8,128)}, u32[]{:S(2)}) copy-start(f32[1,32,16,1024]{3,2,1,0:T(8,128)} %shard_map.118.f0) | copy-start | bytes 6291460
  124.0 19.3 %copy-start.5 = (bf16[8,64,1024]{2,1,0:T(8,128)(2,1)S(1)}, bf16[8,64,1024]{2,1,0:T(8,128)(2,1)}, u32[]{:S(2)}) copy-start(bf16[8,64,1024]{2,1,0:T(8,128)(2,1)} %copy-done.4) | copy-start | bytes 3145732
  150.0 4.4 %collective-permute-start.34 = (bf16[8,24,128]{2,1,0:T(8,128)(2,1)S(1)}, bf16[8,24,128]{2,1,0:T(8,128)(2,1)S(1)}, u32[]{:S(2)}, u32[]{:S(2)}) collective-permute-start(bf16[8,24,128]{2,1,0:T(8,128)(2,1)S(1)} %get-tuple-element.36), channel_id=1, source_target_pairs={{0,32},{2,34},{4,36},{6,38},{1,33},{3,35},{5,37},{7,39},{8,40},{10... | collective-permute-start | bytes 147464 | tf_op jit(solution)/shard_map/ppermute | solution.py:38
  150.9 5.7 %collective-permute-start.35 = (bf16[8,24,128]{2,1,0:T(8,128)(2,1)S(1)}, bf16[8,24,128]{2,1,0:T(8,128)(2,1)S(1)}, u32[]{:S(2)}, u32[]{:S(2)}) collective-permute-start(bf16[8,24,128]{2,1,0:T(8,128)(2,1)S(1)} %get-tuple-element.37), channel_id=1, source_target_pairs={{0,96},{2,98},{4,100},{6,102},{1,97},{3,99},{5,101},{7,103},{8,104... | collective-permute-start | bytes 147464 | tf_op jit(solution)/shard_map/ppermute | solution.py:38
  153.9 5.6 %collective-permute-start.36 = (bf16[8,24,128]{2,1,0:T(8,128)(2,1)S(1)}, bf16[8,24,128]{2,1,0:T(8,128)(2,1)S(1)}, u32[]{:S(2)}, u32[]{:S(2)}) collective-permute-start(bf16[8,24,128]{2,1,0:T(8,128)(2,1)S(1)} %get-tuple-element.38), channel_id=1, source_target_pairs={{0,64},{2,66},{4,68},{6,70},{1,65},{3,67},{5,69},{7,71},{8,72},{10... | collective-permute-start | bytes 147464 | tf_op jit(solution)/shard_map/ppermute | solution.py:38
  159.5 5.4 %collective-permute-start.37 = (f32[2,24,128]{2,1,0:T(8,128)S(1)}, f32[2,24,128]{2,1,0:T(8,128)S(1)}, u32[]{:S(2)}, u32[]{:S(2)}) collective-permute-start(f32[2,24,128]{2,1,0:T(8,128)S(1)} %get-tuple-element.65), channel_id=1, source_target_pairs={{0,8},{2,10},{4,12},{6,14},{1,9},{3,11},{5,13},{7,15},{8,0},{10,2}... | collective-permute-start | bytes 73736 | tf_op jit(solution)/shard_map/ppermute | solution.py:38
  160.2 5.1 %collective-permute-start.38 = (f32[2,24,128]{2,1,0:T(8,128)S(1)}, f32[2,24,128]{2,1,0:T(8,128)S(1)}, u32[]{:S(2)}, u32[]{:S(2)}) collective-permute-start(f32[2,24,128]{2,1,0:T(8,128)S(1)} %get-tuple-element.64), channel_id=1, source_target_pairs={{0,24},{2,26},{4,28},{6,30},{1,25},{3,27},{5,29},{7,31},{8,16},{10... | collective-permute-start | bytes 73736 | tf_op jit(solution)/shard_map/ppermute | solution.py:38
  163.5 5.3 %collective-permute-start.39 = (f32[2,24,128]{2,1,0:T(8,128)S(1)}, f32[2,24,128]{2,1,0:T(8,128)S(1)}, u32[]{:S(2)}, u32[]{:S(2)}) collective-permute-start(f32[2,24,128]{2,1,0:T(8,128)S(1)} %get-tuple-element.63), channel_id=1, source_target_pairs={{0,16},{2,18},{4,20},{6,22},{1,17},{3,19},{5,21},{7,23},{8,24},{10... | collective-permute-start | bytes 73736 | tf_op jit(solution)/shard_map/ppermute | solution.py:38
  168.9 5.3 %collective-permute-start.40 = (f32[24,128]{1,0:T(8,128)S(1)}, f32[24,128]{1,0:T(8,128)S(1)}, u32[]{:S(2)}, u32[]{:S(2)}) collective-permute-start(f32[24,128]{1,0:T(8,128)S(1)} %get-tuple-element.66), channel_id=1, source_target_pairs={{0,1},{2,3},{4,5},{6,7},{1,0},{3,2},{5,4},{7,6},{8,9},{10,11},{12,... | collective-permute-start | bytes 36872 | tf_op jit(solution)/shard_map/ppermute | solution.py:38
  170.1 4.1 %collective-permute-start.41 = (f32[24,128]{1,0:T(8,128)S(1)}, f32[24,128]{1,0:T(8,128)S(1)}, u32[]{:S(2)}, u32[]{:S(2)}) collective-permute-start(f32[24,128]{1,0:T(8,128)S(1)} %get-tuple-element.67), channel_id=1, source_target_pairs={{0,4},{2,6},{4,0},{6,2},{1,5},{3,7},{5,1},{7,3},{8,12},{10,14},{12... | collective-permute-start | bytes 36872 | tf_op jit(solution)/shard_map/ppermute | solution.py:38
  170.6 4.9 %collective-permute-start.42 = (f32[24,128]{1,0:T(8,128)S(1)}, f32[24,128]{1,0:T(8,128)S(1)}, u32[]{:S(2)}, u32[]{:S(2)}) collective-permute-start(f32[24,128]{1,0:T(8,128)S(1)} %get-tuple-element.67), channel_id=1, source_target_pairs={{0,5},{2,7},{4,1},{6,3},{1,4},{3,6},{5,0},{7,2},{8,13},{10,15},{12... | collective-permute-start | bytes 36872 | tf_op jit(solution)/shard_map/ppermute | solution.py:38
  (12 other events, 43.8 us)
